TPU v7x, 32 devices: a whole 2x2x4 slice. The times are simulated.
32 devices in a mesh: seq: 8 (over z, y), head: 4 (over x, core).
Axes of the slice: x: 2, y: 2, z: 4, core: 2. Of those that a mesh axis runs over, the one named last changes fastest.
Arguments:
- queries: bfloat16 [4096, 2048], P('seq', 'head'), may hold values from -8 to 8
- keys: bfloat16 [4096, 1024], P('seq', 'head'), may hold values from -8 to 8
- values: bfloat16 [4096, 1024], P('seq', 'head'), may hold values from -6 to 6
- output_gradient: bfloat16 [4096, 2048], P('seq', 'head'), may hold values from -6 to 6
- key_exponents: int32 [32, 8], P('seq', 'head'), may hold values from -1 to 1
- value_exponents: int32 [32, 8], P('seq', 'head'), may hold values from -1 to 1
- key_matrix: bfloat16 [5376, 1024], P(None, 'head'), may hold values from -0.1875 to 0.1875
- value_matrix: bfloat16 [5376, 1024], P(None, 'head'), may hold values from -0.1875 to 0.1875
Outputs:
- query_grad: bfloat16 [4096, 2048], P('seq', 'head')
- input_grad: bfloat16 [5376, 4096], P('head', 'seq')
All inputs are finite; a program needn't handle non-finite values.
Results may differ from a plain program's by a relative error of at most 0.015.
Values may be sent and summed in bfloat16 or wider, within the bound.
A program may use at most 64 MiB of HBM per device.

v0:
```python
import functools

import jax
import jax.numpy as jnp
from jax import lax
from jax.experimental import pallas as pl
from jax.experimental.pallas import tpu as pltpu
from jax.sharding import PartitionSpec as P

HEAD_SIZE = 128
QUERY_SCALE = 168
ATTEND_WINDOW = 1024
SCALE_BLOCK = 128
LOG2_E = 1.4426950408889634
MESH = pl.DeviceIdType.MESH
F32 = jnp.float32
BF16 = jnp.bfloat16


def power_of_two(exponent):
    return jnp.where(exponent > 0, 2.0, jnp.where(exponent < 0, 0.5, 1.0)).astype(F32)


def contract_last(a, b):
    return lax.dot_general(a, b, (((1,), (1,)), ((), ())), preferred_element_type=F32)


def partner(h, t):
    other, bit = h, 1
    while bit <= t:
        if t & bit:
            other = other + bit - 2 * bit * lax.rem(lax.div(h, bit), 2)
        bit *= 2
    return other


def kernel(
    n, nh, q_ref, k_ref, v_ref, do_ref, ke_ref, ve_ref, wk_ref, wv_ref, dq_ref, out_ref,
    key_true, raw_far, total_own, total_near, smooth, value, smooth_t, dk, dv, grad_out, grad_in,
    scaled, gathered, weights, acc,
    fwd_send, fwd_recv, w_send, w_recv, y_send, y_recv, w_own, g_send, g_recv, far_send, far_recv, s_send, s_recv,
):
    tokens = q_ref.shape[0]
    heads = k_ref.shape[1] // HEAD_SIZE
    D = HEAD_SIZE
    b = lax.axis_index("seq")
    h = lax.axis_index("head")
    rows = out_ref.shape[0]
    own = 2 * tokens

    def cols(g):
        return slice(g * D, (g + 1) * D)

    barrier = pltpu.get_barrier_semaphore()
    for d in (1, 2):
        for to in (lax.rem(b + d, n), lax.rem(b + n - d, n)):
            pl.semaphore_signal(barrier, inc=1, device_id={"seq": to}, device_id_type=MESH)
    for t in range(1, nh):
        pl.semaphore_signal(barrier, inc=1, device_id={"head": partner(h, t)}, device_id_type=MESH)
    pl.semaphore_wait(barrier, 4 + nh - 1)

    def along(src, dst, send, recv, step):
        return pltpu.make_async_remote_copy(
            src_ref=src, dst_ref=dst, send_sem=send, recv_sem=recv,
            device_id={"seq": lax.rem(b + n + step, n)}, device_id_type=MESH,
        )

    def across(src, dst, send, recv, t):
        return pltpu.make_async_remote_copy(
            src_ref=src, dst_ref=dst, send_sem=send, recv_sem=recv,
            device_id={"head": partner(h, t)}, device_id_type=MESH,
        )

    def when_start(condition, copies):
        @pl.when(condition)
        def _():
            for copy in copies:
                copy.start()

    half = rows // 2
    mine = lax.rem(b, 2) * half
    weight_copies, pair_copies = [], []
    for t in list(range(nh - 1, 0, -1)):
        to = partner(h, t)
        for m, ref in enumerate((wk_ref, wv_ref)):
            if t < 3:
                src, dst = ref.at[pl.ds(to * rows, rows), :], weights.at[t, m]
            else:
                src = ref.at[pl.ds(to * rows + mine, half), :]
                dst = weights.at[t, m, pl.ds(mine, half), :]
                pair_copies.append(
                    pltpu.make_async_remote_copy(
                        src_ref=dst, dst_ref=dst, send_sem=y_send.at[t, m], recv_sem=y_recv.at[t, m],
                        device_id={"seq": partner(b, 1)}, device_id_type=MESH,
                    )
                )
            copy = across(src, dst, w_send.at[t, m], w_recv.at[t, m], t)
            copy.start()
            weight_copies.append((t, copy))

    def hand_over(first, last):
        for at in range(first, min(last, len(pair_copies))):
            weight_copies[at][1].wait_recv()
            pair_copies[at].start()

    own_copies = []
    for m, ref in enumerate((wk_ref, wv_ref)):
        copy = pltpu.make_async_copy(ref.at[pl.ds(h * rows, rows), :], weights.at[0, m], w_own.at[m])
        copy.start()
        own_copies.append(copy)

    for j in range(tokens // SCALE_BLOCK):
        at = slice(j * SCALE_BLOCK, (j + 1) * SCALE_BLOCK)
        for g in range(heads):
            key_true[at, cols(g)] = (
                k_ref[at, cols(g)].astype(F32) * power_of_two(ke_ref[j : j + 1, g : g + 1])
            ).astype(BF16)
    key_far = along(key_true, raw_far, fwd_send.at[0], fwd_recv.at[0], 2)
    when_start(b + 2 < n, [key_far])
    keys_own = key_true[...]
    total_own[...] = jnp.broadcast_to(
        jnp.sum(keys_own.astype(F32), axis=0, keepdims=True), total_own.shape
    )
    sum_near = along(total_own, total_near, fwd_send.at[1], fwd_recv.at[1], 1)
    when_start(b + 1 < n, [sum_near])
    for j in range(tokens // SCALE_BLOCK):
        at = slice(j * SCALE_BLOCK, (j + 1) * SCALE_BLOCK)
        for g in range(heads):
            value[g, own + j * SCALE_BLOCK : own + (j + 1) * SCALE_BLOCK, :] = (
                v_ref[at, cols(g)].astype(F32) * power_of_two(ve_ref[j : j + 1, g : g + 1])
            ).astype(BF16)

    def halo(ref, g, kind):
        src = ref.at[g, own : own + tokens]
        at = 2 + 4 * g + 2 * kind
        return (
            along(src, ref.at[g, tokens:own], fwd_send.at[at], fwd_recv.at[at], 1),
            along(src, ref.at[g, 0:tokens], fwd_send.at[at + 1], fwd_recv.at[at + 1], 2),
        )

    halos = [(halo(value, g, 0), halo(smooth, g, 1)) for g in range(heads)]

    def send_halo(copies):
        when_start(b + 2 < n, [copies[1]])
        when_start(b + 1 < n, [copies[0]])

    send_halo(halos[0][0])

    @pl.when(b < 1)
    def _():
        total_near[...] = jnp.zeros_like(total_near)
        for g in range(heads):
            value[g, tokens:own, :] = jnp.zeros((tokens, D), BF16)
            smooth[g, tokens:own, :] = jnp.zeros((tokens, D), BF16)

    @pl.when(b < 2)
    def _():
        raw_far[...] = jnp.zeros_like(raw_far)
        for g in range(heads):
            value[g, 0:tokens, :] = jnp.zeros((tokens, D), BF16)
            smooth[g, 0:tokens, :] = jnp.zeros((tokens, D), BF16)

    row_at = lax.broadcasted_iota(jnp.int32, (tokens, tokens), 0)
    col_at = lax.broadcasted_iota(jnp.int32, (tokens, tokens), 1)
    lower = jnp.where(row_at >= col_at, 1.0, 0.0).astype(BF16)
    running = jnp.dot(lower, keys_own, preferred_element_type=F32)
    place = b * tokens + lax.broadcasted_iota(jnp.int32, (tokens, 1), 0)
    counts = jnp.clip(place + 1, 1, ATTEND_WINDOW).astype(F32)

    @pl.when(b >= 1)
    def _():
        sum_near.wait_recv()

    @pl.when(b >= 2)
    def _():
        key_far.wait_recv()

    far = jnp.dot(lower, raw_far[...], preferred_element_type=F32)
    mean = (running - far + far[tokens - 1 :, :] + total_near[0:1, :]) / counts
    smoothed = (keys_own.astype(F32) - mean).astype(BF16)
    for g in range(heads):
        smooth[g, own : own + tokens, :] = smoothed[:, cols(g)]
    send_halo(halos[0][1])
    for g in range(1, heads):
        send_halo(halos[g][0])
        send_halo(halos[g][1])
    dk[...] = jnp.zeros_like(dk)
    dv[...] = jnp.zeros_like(dv)

    tile = SCALE_BLOCK
    span = ATTEND_WINDOW + tile
    scale = QUERY_SCALE ** (-0.5)
    group = q_ref.shape[1] // (heads * D)
    width = group * tile
    key_row = lax.broadcasted_iota(jnp.int32, (ATTEND_WINDOW, width), 0)
    near_row = lax.broadcasted_iota(jnp.int32, (tile, width), 0)
    lane = lax.rem(lax.broadcasted_iota(jnp.int32, (1, width), 1), tile)

    def far_grad(g, i):
        at = pl.ds(pl.multiple_of(i * tile, tile), tile)
        return along(
            grad_out.at[g, 1, at, :], grad_in.at[g, 1, at, :], far_send.at[g, i], far_recv.at[g, i], -2
        )

    def put_grad(g, d, at, window):
        grad_out[g, d - 1, at, :D] = (dk[g, window, :] * scale).astype(BF16)
        grad_out[g, d - 1, at, D:] = dv[g, window, :].astype(BF16)

    near_copies = []
    for g in range(heads):
        @pl.when(b >= 1)
        def _(g=g):
            for copies in halos[g]:
                copies[0].wait_recv()

        @pl.when(b >= 2)
        def _(g=g):
            for copies in halos[g]:
                copies[1].wait_recv()

        if g == 0:
            hand_over(0, len(pair_copies))
        smooth_t[...] = smooth[g].astype(F32).T.astype(BF16)

        def one_tile(i, carry, g=g):
            begin = pl.multiple_of(i * tile, tile)
            at = pl.ds(begin, tile)
            window = pl.ds(begin, span)
            q = jnp.concatenate([q_ref[at, cols(g * group + u)] for u in range(group)], 0)
            do = jnp.concatenate([do_ref[at, cols(g * group + u)] for u in range(group)], 0)
            keys = smooth[g, window, :]
            values = value[g, window, :]
            scores = contract_last(keys, q)
            first = jnp.maximum(lane + 1, (2 - b) * tokens - begin)
            scores = jnp.concatenate(
                [
                    jnp.where(key_row >= first, scores[:ATTEND_WINDOW], -jnp.inf),
                    jnp.where(near_row <= lane, scores[ATTEND_WINDOW:], -jnp.inf),
                ],
                0,
            )
            highest = jnp.max(scores, axis=0, keepdims=True)
            powers = jnp.exp2((scores - highest) * (scale * LOG2_E))
            shares = powers * (1.0 / jnp.sum(powers, axis=0, keepdims=True))
            rounded = shares.astype(BF16)
            share_grad = contract_last(values, do)
            row_dot = jnp.sum(rounded.astype(F32) * share_grad, axis=0, keepdims=True)
            score_grad = (shares * (share_grad - row_dot)).astype(BF16)
            dv[g, window, :] += jnp.dot(rounded, do, preferred_element_type=F32)
            dk[g, window, :] += jnp.dot(score_grad, q, preferred_element_type=F32)
            dq = jnp.dot(smooth_t[:, window], score_grad, preferred_element_type=F32) * scale
            dq = dq.T.astype(BF16)
            for u in range(group):
                dq_ref[at, cols(g * group + u)] = dq[u * tile : (u + 1) * tile]
            put_grad(g, 2, at, at)
            when_start(b >= 2, [far_grad(g, i)])
            return carry

        lax.fori_loop(0, tokens // tile, one_tile, 0)
        put_grad(g, 1, slice(0, tokens), slice(tokens, own))
        copy = along(grad_out.at[g, 0], grad_in.at[g, 0], g_send.at[g], g_recv.at[g], -1)
        when_start(b >= 1, [copy])
        near_copies.append(copy)

    share_copies = []
    onward = []
    for g in range(heads):
        @pl.when(b + 1 < n)
        def _(g=g):
            near_copies[g].wait_recv()

        @pl.when(b + 1 >= n)
        def _(g=g):
            grad_in[g, 0] = jnp.zeros(grad_in.shape[2:], BF16)

        @pl.when(b + 2 < n)
        def _(g=g):
            for i in range(tokens // tile):
                far_grad(g, i).wait_recv()

        @pl.when(b + 2 >= n)
        def _(g=g):
            grad_in[g, 1] = jnp.zeros(grad_in.shape[2:], BF16)

        for j in range(tokens // SCALE_BLOCK):
            at = slice(j * SCALE_BLOCK, (j + 1) * SCALE_BLOCK)
            here = slice(own + j * SCALE_BLOCK, own + (j + 1) * SCALE_BLOCK)
            for m, (ref, exponent, factor) in enumerate(
                ((dk, ke_ref, scale), (dv, ve_ref, 1.0))
            ):
                whole = ref[g, here, :] * factor
                for d in (1, 2):
                    whole = whole + grad_in[g, d - 1, at, cols(m)].astype(F32)
                scaled[g, at, cols(m)] = (whole * power_of_two(exponent[j : j + 1, g : g + 1])).astype(BF16)
        for t in list(range(2, nh, 2)) + [1]:
            copy = across(
                scaled.at[g], gathered.at[t - 1, g], s_send.at[t - 1, g], s_recv.at[t - 1, g], t
            )
            copy.start()
            share_copies.append((t, copy))
            if t > 1:
                onward.append(
                    (
                        t,
                        copy,
                        across(
                            gathered.at[t - 1, g], gathered.at[t, g],
                            s_send.at[t, g], s_recv.at[t, g], 1,
                        ),
                    )
                )

    chunk = rows // 4

    def product(t, at):
        total = None
        for g in range(heads):
            left = jnp.concatenate([weights[t, 0, at, cols(g)], weights[t, 1, at, cols(g)]], 1)
            right = scaled[g] if t == 0 else gathered[t - 1, g]
            term = contract_last(left, right)
            total = term if total is None else total + term
        return total

    for copy in own_copies:
        copy.wait()
    for t in range(nh):
        if t == 3:
            for copy in pair_copies:
                copy.wait_recv()
        if t in (1, 2):
            for source, copy in weight_copies:
                if source == t:
                    copy.wait_recv()
        if t == 1:
            for source, copy in share_copies:
                if source == 1:
                    copy.wait_recv()
        for source, arrived, copy in onward:
            if source == t:
                arrived.wait_recv()
                copy.start()
            if source == t - 1:
                copy.wait_recv()

        def one_chunk(c, carry, t=t):
            at = pl.ds(pl.multiple_of(c * chunk, 16), chunk)
            total = product(t, at)
            if t > 0:
                total = total + acc[at, :]
            if t < nh - 1:
                acc[at, :] = total
            else:
                out_ref[at, :] = total.astype(BF16)
            return carry

        lax.fori_loop(0, 4, one_chunk, 0)

    @pl.when(b + 1 < n)
    def _():
        sum_near.wait_send()
        for pair in halos:
            for copies in pair:
                copies[0].wait_send()

    @pl.when(b + 2 < n)
    def _():
        key_far.wait_send()
        for pair in halos:
            for copies in pair:
                copies[1].wait_send()

    @pl.when(b >= 1)
    def _():
        for copy in near_copies:
            copy.wait_send()

    @pl.when(b >= 2)
    def _():
        for g in range(heads):
            for i in range(tokens // tile):
                far_grad(g, i).wait_send()

    for _, copy in weight_copies + share_copies:
        copy.wait_send()
    for copy in pair_copies:
        copy.wait_send()
    for _, _, copy in onward:
        copy.wait_send()


def solution(mesh):
    n, nh = mesh.shape["seq"], mesh.shape["head"]

    def local(q, k, v, do, ke, ve, wk, wv):
        tokens, width = k.shape
        heads = width // HEAD_SIZE
        assert ATTEND_WINDOW == 2 * tokens
        rows = wk.shape[0] // nh
        vmem = pl.BlockSpec(memory_space=pltpu.VMEM)
        hbm = pl.BlockSpec(memory_space=pl.ANY)
        dma = pltpu.SemaphoreType.DMA
        return pl.pallas_call(
            functools.partial(kernel, n, nh),
            out_shape=(
                jax.ShapeDtypeStruct(q.shape, BF16),
                jax.ShapeDtypeStruct((rows, tokens), BF16),
            ),
            in_specs=[vmem, vmem, vmem, vmem, vmem, vmem, hbm, hbm],
            out_specs=(vmem, vmem),
            scratch_shapes=[
                pltpu.VMEM((tokens, width), BF16),
                pltpu.VMEM((tokens, width), BF16),
                pltpu.VMEM((8, width), F32),
                pltpu.VMEM((8, width), F32),
                pltpu.VMEM((heads, 3 * tokens, HEAD_SIZE), BF16),
                pltpu.VMEM((heads, 3 * tokens, HEAD_SIZE), BF16),
                pltpu.VMEM((HEAD_SIZE, 3 * tokens), BF16),
                pltpu.VMEM((heads, 3 * tokens, HEAD_SIZE), F32),
                pltpu.VMEM((heads, 3 * tokens, HEAD_SIZE), F32),
                pltpu.VMEM((heads, 2, tokens, 2 * HEAD_SIZE), BF16),
                pltpu.VMEM((heads, 2, tokens, 2 * HEAD_SIZE), BF16),
                pltpu.VMEM((heads, tokens, 2 * HEAD_SIZE), BF16),
                pltpu.VMEM((nh - 1, heads, tokens, 2 * HEAD_SIZE), BF16),
                pltpu.VMEM((nh, 2, rows, width), BF16),
                pltpu.VMEM((rows, tokens), F32),
                dma((2 + 4 * heads,)), dma((2 + 4 * heads,)),
                dma((nh, 2)), dma((nh, 2)), dma((nh, 2)), dma((nh, 2)), dma((2,)),
                dma((heads,)), dma((heads,)),
                dma((heads, tokens // SCALE_BLOCK)), dma((heads, tokens // SCALE_BLOCK)),
                dma((nh - 1, heads)), dma((nh - 1, heads)),
            ],
            compiler_params=pltpu.CompilerParams(
                collective_id=0, has_side_effects=True, vmem_limit_bytes=56 * 2**20
            ),
        )(q, k, v, do, ke, ve, wk, wv)

    in_specs = (P("seq", "head"),) * 6 + (P(None, "head"),) * 2
    out_specs = (P("seq", "head"), P("head", "seq"))
    return jax.shard_map(local, mesh=mesh, in_specs=in_specs, out_specs=out_specs, check_vma=False)
```

profile of v0, /device:TPU:0, one launch (start us, length us, event | category | flops | bytes accessed | tf_op | source)
XLA Modules:
  0.0 77.8 jit_solution(14035921767404260251)
XLA Ops:
  0.6 1.3 %copy.10.ke_ref = s32[4,2]{1,0:T(4,128)} copy(s32[4,2]{0,1:T(2,128)} %param.12) | data formatting | bytes 64 | tf_op args[4]
  2.0 1.3 %copy.11.ve_ref = s32[4,2]{1,0:T(4,128)} copy(s32[4,2]{0,1:T(2,128)} %param.13) | data formatting | bytes 64 | tf_op args[5]
  3.3 70.1 %shard_map.95 = (bf16[512,512]{1,0:T(8,128)(2,1)}, bf16[1344,512]{1,0:T(8,128)(2,1)}) custom-call(bf16[512,512]{1,0:T(8,128)(2,1)} %q_ref.1, bf16[512,256]{1,0:T(8,128)(2,1)} %k_ref.1, bf16[512,256]{1,0:T(8,128)(2,1)} %v_ref.1, bf16[512,512]{1,0:T(8,128)(2,1)} %do_ref.1, s32[4,2]{1,0:T(4,128)} %copy.10.ke_ref, s32[4,2]{1,0:T(4,128)} %copy.11.ve_ref, ...), custom_call_target="tpu_custom_call" | custom-call | tf_op jit(solution)/shard_map/pallas_call | solution.py:402
  73.4 1.9 %copy.14 = bf16[512,512]{1,0:T(8,128)(2,1)} copy(bf16[512,512]{1,0:T(8,128)(2,1)} %get-tuple-element.4) | data formatting | bytes 1048576
  75.3 2.5 %copy.15 = bf16[1344,512]{1,0:T(8,128)(2,1)} copy(bf16[1344,512]{1,0:T(8,128)(2,1)} %get-tuple-element.5) | data formatting | bytes 2752512
where the time goes:
time: 78 us; the launch traced here: 77.8 us
  Pallas kernels  70.1 us (90%)
  local copies, waits for them, and re-layouts  7.04 us (9%)
    pallas_call x1, Pallas kernels, local(): pl.pallas_call(functools.partial(kernel, n, nh), out_shape=(jax.ShapeDtyp...  70.1 us
    unnamed x4, local copies, waits for them, and re-layouts  7.04 us

commit v1 on v0

v1 whole, which is shorter than its diff:
```python
import functools

import jax
import jax.numpy as jnp
from jax import lax
from jax.experimental import pallas as pl
from jax.experimental.pallas import tpu as pltpu
from jax.sharding import PartitionSpec as P

HEAD_SIZE = 128
QUERY_SCALE = 168
ATTEND_WINDOW = 1024
SCALE_BLOCK = 128
LOG2_E = 1.4426950408889634
MESH = pl.DeviceIdType.MESH
F32 = jnp.float32
BF16 = jnp.bfloat16
D = HEAD_SIZE
TILE = SCALE_BLOCK
SPAN = ATTEND_WINDOW + TILE
PIECES = 2
V, S = 0, 1
FAR, NEAR = 0, 1
OVER_Y, OVER_Z = 0, 1


def power_of_two(exponent):
    return jnp.where(exponent > 0, 2.0, jnp.where(exponent < 0, 0.5, 1.0)).astype(F32)


def contract_last(a, b):
    return lax.dot_general(a, b, (((1,), (1,)), ((), ())), preferred_element_type=F32)


def partner(h, t):
    other, bit = h, 1
    while bit <= t:
        if t & bit:
            other = other + bit - 2 * bit * lax.rem(lax.div(h, bit), 2)
        bit *= 2
    return other


def kernel(
    n, nh, q_ref, k_ref, v_ref, do_ref, ke_ref, ve_ref, wk_ref, wv_ref, dq_out, grad_rows,
    k_in, v_in, ke_in, ve_in, q_all, do_all, key_true, raw_far, own_sum, total_own, total_near, smooth, value, smooth_t,
    shares_all, score_all, far_grad, own_grad, grad_out, grad_in, scaled, gathered, weights, acc,
    dq_ref, out_ref, out_sem, in_sem, qd_sem, w_own, kf_send, kf_recv, t_send, t_recv, h_send, h_recv,
    w_send, w_recv, f_down, f_up, f_side, f_recv, c_send, c_recv, g_send, g_recv, s_send, s_recv,
):
    tokens = k_ref.shape[0]
    heads = k_ref.shape[1] // D
    group = q_ref.shape[1] // (heads * D)
    width = group * TILE
    tiles = tokens // TILE
    rows = grad_rows.shape[0]
    own = 2 * tokens
    scale = QUERY_SCALE ** (-0.5)
    b = lax.axis_index("seq")
    h = lax.axis_index("head")
    odd = lax.rem(b, 2) == 1
    even = lax.rem(b, 2) == 0
    colour = lax.rem(lax.rem(b, 2) + lax.div(b, 2), 2)
    crossing = list(range(2, nh))

    def cols(g):
        return slice(g * D, (g + 1) * D)

    loads = [
        pltpu.make_async_copy(k_ref, k_in, in_sem.at[0]),
        pltpu.make_async_copy(v_ref, v_in, in_sem.at[1]),
        pltpu.make_async_copy(ke_ref, ke_in, in_sem.at[2]),
        pltpu.make_async_copy(ve_ref, ve_in, in_sem.at[3]),
    ]
    for copy in loads:
        copy.start()
    head_loads = []
    for g in range(heads):
        for m, (ref, dst) in enumerate(((q_ref, q_all), (do_ref, do_all))):
            for i in range(tiles):
                for u in range(group):
                    head_loads.append(
                        pltpu.make_async_copy(
                            ref.at[i * TILE : (i + 1) * TILE, cols(g * group + u)],
                            dst.at[g, (i * group + u) * TILE : (i * group + u + 1) * TILE, :],
                            qd_sem.at[g, m, i * group + u],
                        )
                    )
    for copy in head_loads:
        copy.start()

    barrier = pltpu.get_barrier_semaphore()

    def greet(step):
        pl.semaphore_signal(
            barrier, inc=1, device_id={"seq": lax.rem(b + n + step, n)}, device_id_type=MESH
        )

    for step in (1, 2):
        pl.when(b + step < n)(lambda: greet(step))
        pl.when(b >= step)(lambda: greet(-step))
    for t in range(1, nh):
        pl.semaphore_signal(barrier, inc=1, device_id={"head": partner(h, t)}, device_id_type=MESH)
    greeted = nh - 1 + jnp.minimum(b, 2) + jnp.minimum(n - 1 - b, 2)

    def when(condition, action):
        pl.when(condition)(action)

    def along(src, dst, send, recv, step):
        return pltpu.make_async_remote_copy(
            src_ref=src, dst_ref=dst, send_sem=send, recv_sem=recv,
            device_id={"seq": lax.rem(b + n + step, n)}, device_id_type=MESH,
        )

    def across(src, dst, send, recv, t):
        return pltpu.make_async_remote_copy(
            src_ref=src, dst_ref=dst, send_sem=send, recv_sem=recv,
            device_id={"head": partner(h, t)}, device_id_type=MESH,
        )

    def when(condition, *steps):
        @pl.when(condition)
        def _():
            for step in steps:
                step()

    half = rows // 2
    part = half // 2
    chunks = [(t, m, q) for q in range(2) for t in crossing for m in range(2)]
    by_down = range(0, len(chunks) // 2)
    by_up = range(len(chunks) // 2, len(chunks) * 3 // 4)
    w_refs = (wk_ref, wv_ref)
    row_0 = b < 2
    row_1 = (b >= 2) & (b < 4)
    top = b + 2 >= n
    below_top = (b + 2 < n) & (b + 4 >= n)

    def held(t, m, q, side):
        return weights.at[t, m, pl.ds(side * half + q * part, part), :]

    def cross_copy(j):
        t, m, q = chunks[j]
        return across(
            w_refs[m].at[pl.ds(partner(h, t) * rows + colour * half + q * part, part), :],
            held(t, m, q, colour), w_send.at[j], w_recv.at[j], t,
        )

    def down_copy(j, side):
        ref = held(*chunks[j], side)
        return along(ref, ref, f_down.at[j], f_recv.at[j], -2)

    def up_copy(j):
        ref = held(*chunks[j], colour)
        return along(ref, ref, f_up.at[j], f_recv.at[j], 2)

    def side_copy(j):
        ref = held(*chunks[j], colour)
        return pltpu.make_async_remote_copy(
            src_ref=ref, dst_ref=ref, send_sem=f_side.at[j], recv_sem=f_recv.at[j],
            device_id={"seq": partner(b, 1)}, device_id_type=MESH,
        )

    def hand(j, action):
        if j in by_down:
            when(b >= 4, lambda: action(down_copy(j, colour)))
            when(below_top, lambda: action(up_copy(j)))
            when(row_0, lambda: action(side_copy(j)))
        elif j in by_up:
            when(b + 2 < n, lambda: action(up_copy(j)))
            when(row_1, lambda: action(down_copy(j, colour)))
        else:
            action(side_copy(j))

    def hand_on(j):
        cross_copy(j).wait_recv()
        hand(j, lambda copy: copy.start())

    core_copies = [
        across(ref.at[pl.ds(partner(h, 1) * rows, rows), :], weights.at[1, m], c_send.at[m], c_recv.at[m], 1)
        for m, ref in enumerate(w_refs)
    ]
    own_copies = [
        pltpu.make_async_copy(ref.at[pl.ds(h * rows, rows), :], weights.at[0, m], w_own.at[m])
        for m, ref in enumerate(w_refs)
    ]

    def key_copy(g):
        return along(key_true.at[g], raw_far.at[g], kf_send.at[g], kf_recv.at[g], 2)

    piece = tokens // PIECES
    halo_refs = (value, smooth)

    def slot(kind, g, base, p):
        return halo_refs[kind].at[g, base + p * piece : base + (p + 1) * piece]

    def far_copy(kind, g, p):
        at = (kind, g, p, FAR)
        return along(slot(kind, g, own, p), slot(kind, g, 0, p), h_send.at[at], h_recv.at[at], 2)

    def near_copy(kind, g, p):
        at = (kind, g, p, NEAR)
        return along(slot(kind, g, own, p), slot(kind, g, tokens, p), h_send.at[at], h_recv.at[at], 1)

    def relay_copy(kind, g, p):
        at = (kind, g, p, NEAR)
        return along(slot(kind, g, 0, p), slot(kind, g, tokens, p), h_send.at[at], h_recv.at[at], -1)

    def send_far(kind, g):
        for p in range(PIECES):
            when(b + 2 < n, lambda: far_copy(kind, g, p).start())

    def send_near(kind, g):
        for p in range(PIECES):
            when(even, lambda: near_copy(kind, g, p).start())

    def relay(kind, g):
        for p in range(PIECES):
            @pl.when(odd & (b >= 2))
            def _():
                far_copy(kind, g, p).wait_recv()
                relay_copy(kind, g, p).start()

    def await_halo(kind, g):
        for p in range(PIECES):
            when(even & (b >= 2), lambda: far_copy(kind, g, p).wait_recv())
            when(b >= 1, lambda: near_copy(kind, g, p).wait_recv())

    def near_sum():
        return along(total_own, total_near, t_send.at[0], t_recv.at[0], 1)

    def rows_of(p, base=0):
        return slice(base + p * piece, base + (p + 1) * piece)

    def grad_copy(m, g, over, p, step):
        at = (m, g, over, rows_of(p))
        return along(grad_out.at[at], grad_in.at[at], g_send.at[m, g, over, p], g_recv.at[m, g, over, p], step)

    def true_keys(g):
        for j in range(tiles):
            at = slice(j * TILE, (j + 1) * TILE)
            key_true[g, at] = (k_in[at, cols(g)].astype(F32) * power_of_two(ke_in[g : g + 1, j : j + 1])).astype(BF16)

    def true_values(g):
        for j in range(tiles):
            at = slice(j * TILE, (j + 1) * TILE)
            value[g, own + j * TILE : own + (j + 1) * TILE] = (
                v_in[at, cols(g)].astype(F32) * power_of_two(ve_in[g : g + 1, j : j + 1])
            ).astype(BF16)

    def sum_keys():
        for g in range(heads):
            total_own[:, cols(g)] = jnp.broadcast_to(
                jnp.sum(key_true[g].astype(F32), axis=0, keepdims=True), (8, D)
            )
        when(b + 1 < n, lambda: near_sum().start())

    def clear():
        @pl.when(b < 1)
        def _():
            total_near[...] = jnp.zeros_like(total_near)
            for g in range(heads):
                value[g, tokens:own, :] = jnp.zeros((tokens, D), BF16)
                smooth[g, tokens:own, :] = jnp.zeros((tokens, D), BF16)

        @pl.when(b < 2)
        def _():
            raw_far[...] = jnp.zeros_like(raw_far)
            for g in range(heads):
                value[g, 0:tokens, :] = jnp.zeros((tokens, D), BF16)
                smooth[g, 0:tokens, :] = jnp.zeros((tokens, D), BF16)
                for m in range(2):
                    grad_in[m, g, OVER_Y] = jnp.zeros((tokens, D), BF16)

        @pl.when(top)
        def _():
            for g in range(heads):
                for m in range(2):
                    grad_in[m, g, OVER_Z] = jnp.zeros((tokens, D), BF16)

        blank = jnp.zeros((TILE, width), BF16)
        for ref in (shares_all, score_all):
            for g in range(heads):
                for i in range(0, tiles, 2):
                    ref[g, i * TILE : (i + 1) * TILE, (i + 1) * width : (i + 2) * width] = blank
                    ref[g, own + (i + 1) * TILE : own + (i + 2) * TILE, i * width : (i + 1) * width] = blank

    row_at = lax.broadcasted_iota(jnp.int32, (tokens, tokens), 0)
    col_at = lax.broadcasted_iota(jnp.int32, (tokens, tokens), 1)
    lower = jnp.where(row_at >= col_at, 1.0, 0.0).astype(BF16)
    place = b * tokens + lax.broadcasted_iota(jnp.int32, (tokens, 1), 0)
    counts = jnp.clip(place + 1, 1, ATTEND_WINDOW).astype(F32)

    def running_keys(g):
        own_sum[g] = jnp.dot(lower, key_true[g], preferred_element_type=F32)

    def smooth_keys(g):
        when(b >= 2, lambda: key_copy(g).wait_recv())
        far = jnp.dot(lower, raw_far[g], preferred_element_type=F32)
        mean = (own_sum[g] - far + far[tokens - 1 :, :] + total_near[0:1, cols(g)]) / counts
        smooth[g, own : own + tokens, :] = (key_true[g].astype(F32) - mean).astype(BF16)
        send_far(S, g)
        send_near(S, g)

    near_row = lax.broadcasted_iota(jnp.int32, (TILE, width), 0)
    lane = lax.rem(lax.broadcasted_iota(jnp.int32, (1, width), 1), TILE)

    def attend(g):
        def one_tile(i, carry):
            begin = pl.multiple_of(i * TILE, TILE)
            window = pl.ds(begin, SPAN)
            lanes = pl.ds(pl.multiple_of(i * width, width), width)
            scores = contract_last(smooth[g, window, :], q_all[g, lanes, :])
            blocks = []
            for j in range(SPAN // TILE):
                block = scores[j * TILE : (j + 1) * TILE]
                if j == 0:
                    block = jnp.where(near_row > lane, block, -jnp.inf)
                if j == ATTEND_WINDOW // TILE:
                    block = jnp.where(near_row <= lane, block, -jnp.inf)
                else:
                    block = jnp.where(i + j >= (2 - b) * tiles, block, -jnp.inf)
                blocks.append(block)
            scores = jnp.concatenate(blocks, 0)
            highest = jnp.max(scores, axis=0, keepdims=True)
            powers = jnp.exp2((scores - highest) * (scale * LOG2_E))
            shares = powers * (1.0 / jnp.sum(powers, axis=0, keepdims=True))
            shares_all[g, window, lanes] = shares.astype(BF16)
            return carry

        lax.fori_loop(0, tiles, one_tile, 0)

    def differentiate(g):
        def one_tile(i, carry):
            begin = pl.multiple_of(i * TILE, TILE)
            window = pl.ds(begin, SPAN)
            lanes = pl.ds(pl.multiple_of(i * width, width), width)
            share_grad = contract_last(value[g, window, :], do_all[g, lanes, :])
            shares = shares_all[g, window, lanes].astype(F32)
            row_dot = jnp.sum(shares * share_grad, axis=0, keepdims=True)
            score_all[g, window, lanes] = (shares * (share_grad - row_dot)).astype(BF16)
            return carry

        lax.fori_loop(0, tiles, one_tile, 0)

    def key_grads(m, g, at, lanes):
        if m == 0:
            return jnp.dot(score_all[g, at, lanes], q_all[g, lanes, :], preferred_element_type=F32) * scale
        return jnp.dot(shares_all[g, at, lanes], do_all[g, lanes, :], preferred_element_type=F32)

    def near_grads(m, g):
        for p in range(PIECES):
            grads = key_grads(m, g, rows_of(p, tokens), slice(0, group * tokens))
            grad_out[m, g, OVER_Y, rows_of(p)] = grads.astype(BF16)

    def send_near_grads(m, g):
        for p in range(PIECES):
            when(even & (b >= 2), lambda: grad_copy(m, g, OVER_Y, p, 1).start())
            when(odd, lambda: grad_copy(m, g, OVER_Y, p, -1).start())

    def far_grads(m, g):
        for p in range(PIECES):
            grads = key_grads(m, g, rows_of(p), slice(0, (p + 1) * group * piece))
            far_grad[m, g, rows_of(p)] = grads

            @pl.when(even & (b >= 2))
            def _():
                grad_out[m, g, OVER_Z, rows_of(p)] = far_grad[m, g, rows_of(p)].astype(BF16)
                grad_copy(m, g, OVER_Z, p, -2).start()

    def join_grads(m, g):
        for p in range(PIECES):
            @pl.when(odd & (b >= 2))
            def _():
                grad_copy(m, g, OVER_Y, p, 1).wait_recv()
                both = far_grad[m, g, rows_of(p)] + grad_in[m, g, OVER_Y, rows_of(p)].astype(F32)
                grad_out[m, g, OVER_Z, rows_of(p)] = both.astype(BF16)
                grad_copy(m, g, OVER_Z, p, -2).start()

    def own_grads(m, g):
        for p in range(PIECES):
            own_grad[m, g, rows_of(p)] = key_grads(
                m, g, rows_of(p, own), slice(p * group * piece, group * tokens)
            )

    def query_grads(g):
        smooth_t[...] = smooth[g].astype(F32).T.astype(BF16)
        for i in range(tiles):
            window = slice(i * TILE, i * TILE + SPAN)
            dq = jnp.dot(
                smooth_t[:, window], score_all[g, window, i * width : (i + 1) * width],
                preferred_element_type=F32,
            ) * scale
            dq = dq.T.astype(BF16)
            for u in range(group):
                dq_ref[i * TILE : (i + 1) * TILE, cols(g * group + u)] = dq[u * TILE : (u + 1) * TILE]

    def share_copy(m, g, p, t):
        return across(
            scaled.at[m, g, rows_of(p)], gathered.at[t - 1, m, g, rows_of(p)],
            s_send.at[t - 1, m, g, p], s_recv.at[t - 1, m, g, p], t,
        )

    def onward_copy(m, g, p, t):
        return across(
            gathered.at[t - 1, m, g, rows_of(p)], gathered.at[t, m, g, rows_of(p)],
            s_send.at[t, m, g, p], s_recv.at[t, m, g, p], 1,
        )

    far_steps = list(range(2, nh, 2))

    def finish(m, g):
        exponent = (ke_in, ve_in)[m]
        for p in range(PIECES):
            when(even, lambda: grad_copy(m, g, OVER_Y, p, -1).wait_recv())
            when(b + 2 < n, lambda: grad_copy(m, g, OVER_Z, p, -2).wait_recv())
            for r in range(p * tiles // PIECES, (p + 1) * tiles // PIECES):
                at = slice(r * TILE, (r + 1) * TILE)
                whole = own_grad[m, g, at] + grad_in[m, g, OVER_Z, at].astype(F32)
                whole = whole + jnp.where(even, grad_in[m, g, OVER_Y, at].astype(F32), 0.0)
                scaled[m, g, at] = (whole * power_of_two(exponent[g : g + 1, r : r + 1])).astype(BF16)
            for t in far_steps + [1]:
                share_copy(m, g, p, t).start()

    def pass_on(m, g):
        for p in range(PIECES):
            for t in far_steps:
                share_copy(m, g, p, t).wait_recv()
                onward_copy(m, g, p, t).start()

    def await_core(g):
        for m in range(2):
            for p in range(PIECES):
                share_copy(m, g, p, 1).wait_recv()

    def await_onward(g):
        for m in range(2):
            for p in range(PIECES):
                for t in far_steps:
                    onward_copy(m, g, p, t).wait_recv()

    chunk = rows // 4

    def row_copy(c):
        at = pl.ds(pl.multiple_of(c * chunk, 16), chunk)
        return pltpu.make_async_copy(out_ref.at[at, :], grad_rows.at[at, :], out_sem.at[c])

    def query_copy():
        return pltpu.make_async_copy(dq_ref, dq_out, out_sem.at[4])

    def product(ts, g, fresh, last):
        def one_chunk(c, carry):
            at = pl.ds(pl.multiple_of(c * chunk, 16), chunk)
            total = None if fresh else acc[at, :]
            for t in ts:
                left = jnp.concatenate([weights[t, 0, at, cols(g)], weights[t, 1, at, cols(g)]], 1)
                if t == 0:
                    right = jnp.concatenate([scaled[0, g], scaled[1, g]], 1)
                else:
                    right = jnp.concatenate([gathered[t - 1, 0, g], gathered[t - 1, 1, g]], 1)
                term = contract_last(left, right)
                total = term if total is None else total + term
            if last:
                out_ref[at, :] = total.astype(BF16)
                row_copy(c).start()
            else:
                acc[at, :] = total
            return carry

        lax.fori_loop(0, 4, one_chunk, 0)

    pl.semaphore_wait(barrier, greeted)
    for copy in loads: copy.wait()
    for j in range(len(chunks)): cross_copy(j).start()
    for g in range(heads): true_keys(g)
    sum_keys()
    for g in range(heads): when(b + 2 < n, lambda: key_copy(g).start())
    for g in range(heads):
        true_values(g)
        send_near(V, g)
    for copy in core_copies + own_copies: copy.start()
    clear()
    for g in range(heads): running_keys(g)
    when(b >= 1, lambda: near_sum().wait_recv())
    smooth_keys(0)
    smooth_keys(1)
    for g in range(heads): send_far(V, g)
    for copy in head_loads: copy.wait()
    hand_on(0)
    relay(S, 0)
    await_halo(S, 0)
    attend(0)
    relay(S, 1)
    hand_on(1)
    await_halo(S, 1)
    attend(1)
    relay(V, 0)
    hand_on(2)
    near_grads(1, 0)
    near_grads(1, 1)
    relay(V, 1)
    send_near_grads(1, 0)
    send_near_grads(1, 1)
    far_grads(1, 0)
    far_grads(1, 1)
    hand_on(3)
    await_halo(V, 0)
    differentiate(0)
    near_grads(0, 0)
    send_near_grads(0, 0)
    far_grads(0, 0)
    hand_on(4)
    await_halo(V, 1)
    differentiate(1)
    near_grads(0, 1)
    send_near_grads(0, 1)
    join_grads(1, 0)
    far_grads(0, 1)
    own_grads(1, 0)
    join_grads(1, 1)
    hand_on(5)
    own_grads(1, 1)
    own_grads(0, 0)
    own_grads(0, 1)
    join_grads(0, 0)
    finish(1, 0)
    hand_on(6)
    query_grads(0)
    join_grads(0, 1)
    finish(1, 1)
    finish(0, 0)
    hand_on(7)
    for copy in own_copies: copy.wait()
    for copy in core_copies: copy.wait_recv()
    await_core(0)
    product((0, 1), 0, True, False)
    finish(0, 1)
    query_grads(1)
    query_copy().start()
    for m in (1, 0): pass_on(m, 0)
    await_core(1)
    product((0, 1), 1, False, False)
    for j in range(len(chunks)): down_copy(j, 1 - colour).wait_recv()
    await_onward(0)
    product(crossing, 0, False, False)
    for m in (1, 0): pass_on(m, 1)
    await_onward(1)
    product(crossing, 1, False, True)

    query_copy().wait()
    for c in range(4):
        row_copy(c).wait()
    when(b + 1 < n, lambda: near_sum().wait_send())
    for g in range(heads):
        when(b + 2 < n, lambda: key_copy(g).wait_send())
        for p in range(PIECES):
            for kind in (V, S):
                when(b + 2 < n, lambda: far_copy(kind, g, p).wait_send())
                when(even | (b >= 2), lambda: near_copy(kind, g, p).wait_send())
            for m in range(2):
                when(odd | (b >= 2), lambda: grad_copy(m, g, OVER_Y, p, 1).wait_send())
                when(b >= 2, lambda: grad_copy(m, g, OVER_Z, p, -2).wait_send())
                for t in far_steps + [1]:
                    share_copy(m, g, p, t).wait_send()
                for t in far_steps:
                    onward_copy(m, g, p, t).wait_send()
    for j in range(len(chunks)):
        cross_copy(j).wait_send()
        hand(j, lambda copy: copy.wait_send())
    for copy in core_copies:
        copy.wait_send()


def solution(mesh):
    n, nh = mesh.shape["seq"], mesh.shape["head"]
    assert n % 2 == 0 and n >= 4

    def local(q, k, v, do, ke, ve, wk, wv):
        tokens, width = k.shape
        heads = width // HEAD_SIZE
        group = q.shape[1] // width
        tiles = tokens // TILE
        assert ATTEND_WINDOW == 2 * tokens
        rows = wk.shape[0] // nh
        n_chunks = 4 * (nh - 2)
        hbm = pl.BlockSpec(memory_space=pltpu.HBM)
        dma = pltpu.SemaphoreType.DMA
        return pl.pallas_call(
            functools.partial(kernel, n, nh),
            out_shape=(
                pltpu.VMEM(q.shape, BF16),
                pltpu.VMEM((rows, tokens), BF16),
            ),
            in_specs=[hbm] * 8,
            out_specs=(pl.BlockSpec(memory_space=pl.ANY),) * 2,
            scratch_shapes=[
                pltpu.VMEM((tokens, width), BF16),
                pltpu.VMEM((tokens, width), BF16),
                pltpu.VMEM((heads, tiles), jnp.int32),
                pltpu.VMEM((heads, tiles), jnp.int32),
                pltpu.VMEM((heads, group * tokens, D), BF16),
                pltpu.VMEM((heads, group * tokens, D), BF16),
                pltpu.VMEM((heads, tokens, D), BF16),
                pltpu.VMEM((heads, tokens, D), BF16),
                pltpu.VMEM((heads, tokens, D), F32),
                pltpu.VMEM((8, width), F32),
                pltpu.VMEM((8, width), F32),
                pltpu.VMEM((heads, 3 * tokens, D), BF16),
                pltpu.VMEM((heads, 3 * tokens, D), BF16),
                pltpu.VMEM((D, 3 * tokens), BF16),
                pltpu.VMEM((heads, 3 * tokens, group * tokens), BF16),
                pltpu.VMEM((heads, 3 * tokens, group * tokens), BF16),
                pltpu.VMEM((2, heads, tokens, D), F32),
                pltpu.VMEM((2, heads, tokens, D), F32),
                pltpu.VMEM((2, heads, 2, tokens, D), BF16),
                pltpu.VMEM((2, heads, 2, tokens, D), BF16),
                pltpu.VMEM((2, heads, tokens, D), BF16),
                pltpu.VMEM((nh - 1, 2, heads, tokens, D), BF16),
                pltpu.VMEM((nh, 2, rows, width), BF16),
                pltpu.VMEM((rows, tokens), F32),
                pltpu.VMEM(q.shape, BF16),
                pltpu.VMEM((rows, tokens), BF16),
                dma((5,)),
                dma((4,)), dma((heads, 2, group * tiles)), dma((2,)),
                dma((heads,)), dma((heads,)), dma((1,)), dma((1,)),
                dma((2, heads, PIECES, 2)), dma((2, heads, PIECES, 2)),
                dma((n_chunks,)), dma((n_chunks,)),
                dma((n_chunks,)), dma((n_chunks,)), dma((n_chunks,)), dma((n_chunks,)),
                dma((2,)), dma((2,)),
                dma((2, heads, 2, PIECES)), dma((2, heads, 2, PIECES)),
                dma((nh - 1, 2, heads, PIECES)), dma((nh - 1, 2, heads, PIECES)),
            ],
            compiler_params=pltpu.CompilerParams(
                collective_id=0, has_side_effects=True, vmem_limit_bytes=48 * 2**20
            ),
        )(*[pltpu.with_memory_space_constraint(x, pltpu.HBM) for x in (q, k, v, do, ke.T, ve.T, wk, wv)])

    in_specs = (P("seq", "head"),) * 6 + (P(None, "head"),) * 2
    out_specs = (P("seq", "head"), P("head", "seq"))
    return jax.shard_map(local, mesh=mesh, in_specs=in_specs, out_specs=out_specs, check_vma=False)
```

time: 78 us -> 58.9 us (0.76); the launches traced: 77.8 us -> 57.7 us
  Pallas kernels: 70.1 us -> 55.2 us
  local copies, waits for them, and re-layouts: 7.04 us -> 1.87 us
    pallas_call x1, Pallas kernels: 70.1 us -> 55.2 us  [local(): pl.pallas_call(functools.partial(kernel, n, nh), out_shape=(pltpu.VMEM(q....]
    unnamed x4 -> x2, local copies, waits for them, and re-layouts: 7.04 us -> 1.87 us
where the time goes in v1:
time: 58.9 us; the launch traced here: 57.7 us
  Pallas kernels  55.2 us (94%)
  local copies, waits for them, and re-layouts  1.87 us (3%)
  between operations  0.64 us (1%)
    pallas_call x1, Pallas kernels, local(): pl.pallas_call(functools.partial(kernel, n, nh), out_shape=(pltpu.VMEM(q....  55.2 us
    unnamed x2, local copies, waits for them, and re-layouts  1.87 us

profile of v1, /device:TPU:0, one launch (start us, length us, event | category | flops | bytes accessed | tf_op | source)
XLA Modules:
  0.0 57.7 jit_solution(13040630583065215670)
XLA Ops:
  0.6 55.2 %shard_map.95 = (bf16[512,512]{1,0:T(8,128)(2,1)S(1)}, bf16[1344,512]{1,0:T(8,128)(2,1)S(1)}) custom-call(bf16[512,512]{1,0:T(8,128)(2,1)} %q_ref.1, bf16[512,256]{1,0:T(8,128)(2,1)} %k_ref.1, bf16[512,256]{1,0:T(8,128)(2,1)} %v_ref.1, bf16[512,512]{1,0:T(8,128)(2,1)} %do_ref.1, s32[2,4]{1,0:T(2,128)} %bitcast.2, s32[2,4]{1,0:T(2,128)} %bitcast.3, ...), custom_call_target="tpu_custom_call" | custom-call | tf_op jit(solution)/shard_map/pallas_call | solution.py:587
  55.8 0.8 %copy.12 = bf16[512,512]{1,0:T(8,128)(2,1)} copy(bf16[512,512]{1,0:T(8,128)(2,1)S(1)} %get-tuple-element.2) | data formatting | bytes 1048576
  56.6 1.1 %copy.13 = bf16[1344,512]{1,0:T(8,128)(2,1)} copy(bf16[1344,512]{1,0:T(8,128)(2,1)S(1)} %get-tuple-element.3) | data formatting | bytes 2752512

commit v2 on v1

--- a/solution.py
+++ b/solution.py
@@ -12,6 +12,7 @@
 ATTEND_WINDOW = 1024
 SCALE_BLOCK = 128
 LOG2_E = 1.4426950408889634
+LOWEST = -1e30
 MESH = pl.DeviceIdType.MESH
 F32 = jnp.float32
 BF16 = jnp.bfloat16
@@ -44,9 +45,9 @@
 def kernel(
     n, nh, q_ref, k_ref, v_ref, do_ref, ke_ref, ve_ref, wk_ref, wv_ref, dq_out, grad_rows,
     k_in, v_in, ke_in, ve_in, q_all, do_all, key_true, raw_far, own_sum, total_own, total_near, smooth, value, smooth_t,
-    shares_all, score_all, far_grad, own_grad, grad_out, grad_in, scaled, gathered, weights, acc,
+    shares_all, score_all, stats, do_part, far_grad, own_grad, grad_out, grad_in, scaled, gathered, weights, acc,
     dq_ref, out_ref, out_sem, in_sem, qd_sem, w_own, kf_send, kf_recv, t_send, t_recv, h_send, h_recv,
-    w_send, w_recv, f_down, f_up, f_side, f_recv, c_send, c_recv, g_send, g_recv, s_send, s_recv,
+    w_send, w_recv, f_send, f_recv, c_send, c_recv, g_send, g_recv, s_send, s_recv,
 ):
     tokens = k_ref.shape[0]
     heads = k_ref.shape[1] // D
@@ -83,7 +84,7 @@
                         pltpu.make_async_copy(
                             ref.at[i * TILE : (i + 1) * TILE, cols(g * group + u)],
                             dst.at[g, (i * group + u) * TILE : (i * group + u + 1) * TILE, :],
-                            qd_sem.at[g, m, i * group + u],
+                            qd_sem.at[g, m],
                         )
                     )
     for copy in head_loads:
@@ -129,6 +130,7 @@
     chunks = [(t, m, q) for q in range(2) for t in crossing for m in range(2)]
     by_down = range(0, len(chunks) // 2)
     by_up = range(len(chunks) // 2, len(chunks) * 3 // 4)
+    late = len(chunks) - 2
     w_refs = (wk_ref, wv_ref)
     row_0 = b < 2
     row_1 = (b >= 2) & (b < 4)
@@ -142,21 +144,21 @@
         t, m, q = chunks[j]
         return across(
             w_refs[m].at[pl.ds(partner(h, t) * rows + colour * half + q * part, part), :],
-            held(t, m, q, colour), w_send.at[j], w_recv.at[j], t,
+            held(t, m, q, colour), w_send.at[0], w_recv.at[j], t,
         )
 
     def down_copy(j, side):
         ref = held(*chunks[j], side)
-        return along(ref, ref, f_down.at[j], f_recv.at[j], -2)
+        return along(ref, ref, f_send.at[j, 0], f_recv.at[j], -2)
 
     def up_copy(j):
         ref = held(*chunks[j], colour)
-        return along(ref, ref, f_up.at[j], f_recv.at[j], 2)
+        return along(ref, ref, f_send.at[j, 1], f_recv.at[j], 2)
 
     def side_copy(j):
         ref = held(*chunks[j], colour)
         return pltpu.make_async_remote_copy(
-            src_ref=ref, dst_ref=ref, send_sem=f_side.at[j], recv_sem=f_recv.at[j],
+            src_ref=ref, dst_ref=ref, send_sem=f_send.at[j, 0], recv_sem=f_recv.at[j],
             device_id={"seq": partner(b, 1)}, device_id_type=MESH,
         )
 
@@ -167,9 +169,18 @@
             when(row_0, lambda: action(side_copy(j)))
         elif j in by_up:
             when(b + 2 < n, lambda: action(up_copy(j)))
-            when(row_1, lambda: action(down_copy(j, colour)))
+            if j == by_up[0]:
+                when(row_1, lambda: action(down_copy(j, colour)))
+            else:
+                when(row_0, lambda: action(side_copy(j)))
+        elif j == late:
+            when(b >= 2, lambda: action(side_copy(j)))
         else:
             action(side_copy(j))
+
+    def hand_late(action):
+        ref = held(*chunks[late], colour)
+        when(row_1, lambda: action(along(ref, ref, f_send.at[late, 1], f_recv.at[late], -2)))
 
     def hand_on(j):
         cross_copy(j).wait_recv()
@@ -195,15 +206,15 @@
 
     def far_copy(kind, g, p):
         at = (kind, g, p, FAR)
-        return along(slot(kind, g, own, p), slot(kind, g, 0, p), h_send.at[at], h_recv.at[at], 2)
+        return along(slot(kind, g, own, p), slot(kind, g, 0, p), h_send.at[FAR], h_recv.at[at], 2)
 
     def near_copy(kind, g, p):
         at = (kind, g, p, NEAR)
-        return along(slot(kind, g, own, p), slot(kind, g, tokens, p), h_send.at[at], h_recv.at[at], 1)
+        return along(slot(kind, g, own, p), slot(kind, g, tokens, p), h_send.at[NEAR], h_recv.at[at], 1)
 
     def relay_copy(kind, g, p):
         at = (kind, g, p, NEAR)
-        return along(slot(kind, g, 0, p), slot(kind, g, tokens, p), h_send.at[at], h_recv.at[at], -1)
+        return along(slot(kind, g, 0, p), slot(kind, g, tokens, p), h_send.at[NEAR], h_recv.at[at], -1)
 
     def send_far(kind, g):
         for p in range(PIECES):
@@ -220,20 +231,27 @@
                 far_copy(kind, g, p).wait_recv()
                 relay_copy(kind, g, p).start()
 
-    def await_halo(kind, g):
+    def await_far(kind, g):
         for p in range(PIECES):
             when(even & (b >= 2), lambda: far_copy(kind, g, p).wait_recv())
+
+    def await_near(kind, g):
+        for p in range(PIECES):
             when(b >= 1, lambda: near_copy(kind, g, p).wait_recv())
 
     def near_sum():
         return along(total_own, total_near, t_send.at[0], t_recv.at[0], 1)
 
+    def await_heads(g):
+        for m, ref in enumerate((q_all, do_all)):
+            pltpu.make_async_copy(ref.at[g], ref.at[g], qd_sem.at[g, m]).wait()
+
     def rows_of(p, base=0):
         return slice(base + p * piece, base + (p + 1) * piece)
 
     def grad_copy(m, g, over, p, step):
         at = (m, g, over, rows_of(p))
-        return along(grad_out.at[at], grad_in.at[at], g_send.at[m, g, over, p], g_recv.at[m, g, over, p], step)
+        return along(grad_out.at[at], grad_in.at[at], g_send.at[over], g_recv.at[m, g, over, p], step)
 
     def true_keys(g):
         for j in range(tiles):
@@ -301,55 +319,75 @@
         send_far(S, g)
         send_near(S, g)
 
-    near_row = lax.broadcasted_iota(jnp.int32, (TILE, width), 0)
+    row = lax.broadcasted_iota(jnp.int32, (TILE, width), 0)
     lane = lax.rem(lax.broadcasted_iota(jnp.int32, (1, width), 1), TILE)
-
-    def attend(g):
-        def one_tile(i, carry):
-            begin = pl.multiple_of(i * TILE, TILE)
-            window = pl.ds(begin, SPAN)
-            lanes = pl.ds(pl.multiple_of(i * width, width), width)
-            scores = contract_last(smooth[g, window, :], q_all[g, lanes, :])
-            blocks = []
-            for j in range(SPAN // TILE):
-                block = scores[j * TILE : (j + 1) * TILE]
-                if j == 0:
-                    block = jnp.where(near_row > lane, block, -jnp.inf)
-                if j == ATTEND_WINDOW // TILE:
-                    block = jnp.where(near_row <= lane, block, -jnp.inf)
-                else:
-                    block = jnp.where(i + j >= (2 - b) * tiles, block, -jnp.inf)
-                blocks.append(block)
-            scores = jnp.concatenate(blocks, 0)
-            highest = jnp.max(scores, axis=0, keepdims=True)
+    unit = jnp.where(
+        lax.broadcasted_iota(jnp.int32, (TILE, TILE), 0) == lax.broadcasted_iota(jnp.int32, (TILE, TILE), 1), 1.0, 0.0
+    )
+
+    def lanes_of(i):
+        return slice(i * width, (i + 1) * width)
+
+    def keys_of(part, i):
+        return (slice(i * TILE, tokens), slice(tokens, own), slice(own, own + (i + 1) * TILE))[part]
+
+    def attend(g, part):
+        for i in range(tiles):
+            at, lanes = keys_of(part, i), lanes_of(i)
+            scores = contract_last(smooth[g, at, :], q_all[g, lanes, :])
+            if part == 0:
+                edge = jnp.where(row > lane, scores[:TILE], -jnp.inf)
+                scores = edge if i == tiles - 1 else jnp.concatenate([edge, scores[TILE:]], 0)
+            if part == 2:
+                edge = jnp.where(row <= lane, scores[i * TILE :], -jnp.inf)
+                scores = edge if i == 0 else jnp.concatenate([scores[: i * TILE], edge], 0)
+            highest = jnp.maximum(jnp.max(scores, axis=0, keepdims=True), LOWEST)
             powers = jnp.exp2((scores - highest) * (scale * LOG2_E))
-            shares = powers * (1.0 / jnp.sum(powers, axis=0, keepdims=True))
-            shares_all[g, window, lanes] = shares.astype(BF16)
-            return carry
-
-        lax.fori_loop(0, tiles, one_tile, 0)
+            shares_all[g, at, lanes] = powers.astype(BF16)
+            stats[g, part, 0:1, lanes] = highest
+            stats[g, part, 1:2, lanes] = jnp.sum(powers, axis=0, keepdims=True)
+
+    def combine(g):
+        present = (b >= 2, b >= 1, b >= 0)
+        tops = [jnp.where(here, stats[g, part, 0:1, :], LOWEST) for part, here in enumerate(present)]
+        highest = jnp.maximum(jnp.maximum(tops[0], tops[1]), tops[2])
+        powers = [
+            jnp.where(here, jnp.exp2((top - highest) * (scale * LOG2_E)), 0.0) for top, here in zip(tops, present)
+        ]
+        total = sum(power * stats[g, part, 1:2, :] for part, power in enumerate(powers))
+        inverse = 1.0 / total
+        for part in range(3):
+            factor = powers[part] * inverse
+            stats[g, part, 0:1, :] = factor.astype(BF16).astype(F32)
+            for k in range(group * tiles):
+                at = slice(k * TILE, (k + 1) * TILE)
+                spread = (unit * factor[:, at]).astype(BF16)
+                do_part[g, part, at, :] = jnp.dot(
+                    spread, do_all[g, at, :], preferred_element_type=F32
+                ).astype(BF16)
 
     def differentiate(g):
-        def one_tile(i, carry):
-            begin = pl.multiple_of(i * TILE, TILE)
-            window = pl.ds(begin, SPAN)
-            lanes = pl.ds(pl.multiple_of(i * width, width), width)
-            share_grad = contract_last(value[g, window, :], do_all[g, lanes, :])
-            shares = shares_all[g, window, lanes].astype(F32)
-            row_dot = jnp.sum(shares * share_grad, axis=0, keepdims=True)
-            score_all[g, window, lanes] = (shares * (share_grad - row_dot)).astype(BF16)
-            return carry
-
-        lax.fori_loop(0, tiles, one_tile, 0)
-
-    def key_grads(m, g, at, lanes):
+        for i in range(tiles):
+            lanes = lanes_of(i)
+            row_dot, parts = 0.0, []
+            for part in range(3):
+                at = keys_of(part, i)
+                share_grad = contract_last(value[g, at, :], do_part[g, part, lanes, :])
+                shares = shares_all[g, at, lanes].astype(F32)
+                row_dot = row_dot + jnp.sum(shares * share_grad, axis=0, keepdims=True)
+                parts.append((at, shares, share_grad))
+            for part, (at, shares, share_grad) in enumerate(parts):
+                shift = row_dot * stats[g, part, 0:1, lanes]
+                score_all[g, at, lanes] = (shares * (share_grad - shift)).astype(BF16)
+
+    def key_grads(m, g, part, at, lanes):
         if m == 0:
             return jnp.dot(score_all[g, at, lanes], q_all[g, lanes, :], preferred_element_type=F32) * scale
-        return jnp.dot(shares_all[g, at, lanes], do_all[g, lanes, :], preferred_element_type=F32)
+        return jnp.dot(shares_all[g, at, lanes], do_part[g, part, lanes, :], preferred_element_type=F32)
 
     def near_grads(m, g):
         for p in range(PIECES):
-            grads = key_grads(m, g, rows_of(p, tokens), slice(0, group * tokens))
+            grads = key_grads(m, g, 1, rows_of(p, tokens), slice(0, group * tokens))
             grad_out[m, g, OVER_Y, rows_of(p)] = grads.astype(BF16)
 
     def send_near_grads(m, g):
@@ -359,7 +397,7 @@
 
     def far_grads(m, g):
         for p in range(PIECES):
-            grads = key_grads(m, g, rows_of(p), slice(0, (p + 1) * group * piece))
+            grads = key_grads(m, g, 0, rows_of(p), slice(0, (p + 1) * group * piece))
             far_grad[m, g, rows_of(p)] = grads
 
             @pl.when(even & (b >= 2))
@@ -379,7 +417,7 @@
     def own_grads(m, g):
         for p in range(PIECES):
             own_grad[m, g, rows_of(p)] = key_grads(
-                m, g, rows_of(p, own), slice(p * group * piece, group * tokens)
+                m, g, 2, rows_of(p, own), slice(p * group * piece, group * tokens)
             )
 
     def query_grads(g):
@@ -395,16 +433,11 @@
                 dq_ref[i * TILE : (i + 1) * TILE, cols(g * group + u)] = dq[u * TILE : (u + 1) * TILE]
 
     def share_copy(m, g, p, t):
-        return across(
-            scaled.at[m, g, rows_of(p)], gathered.at[t - 1, m, g, rows_of(p)],
-            s_send.at[t - 1, m, g, p], s_recv.at[t - 1, m, g, p], t,
-        )
-
-    def onward_copy(m, g, p, t):
-        return across(
-            gathered.at[t - 1, m, g, rows_of(p)], gathered.at[t, m, g, rows_of(p)],
-            s_send.at[t, m, g, p], s_recv.at[t, m, g, p], 1,
-        )
+        at = (m, g) if p is None else (m, g, rows_of(p))
+        return across(scaled.at[at], gathered.at[(t - 1,) + at], s_send.at[t - 1], s_recv.at[t - 1, m, g], t)
+
+    def onward_copy(m, g, t):
+        return across(gathered.at[t - 1, m, g], gathered.at[t, m, g], s_send.at[t], s_recv.at[t, m, g], 1)
 
     far_steps = list(range(2, nh, 2))
 
@@ -422,21 +455,18 @@
                 share_copy(m, g, p, t).start()
 
     def pass_on(m, g):
-        for p in range(PIECES):
-            for t in far_steps:
-                share_copy(m, g, p, t).wait_recv()
-                onward_copy(m, g, p, t).start()
+        for t in far_steps:
+            share_copy(m, g, None, t).wait_recv()
+            onward_copy(m, g, t).start()
 
     def await_core(g):
         for m in range(2):
-            for p in range(PIECES):
-                share_copy(m, g, p, 1).wait_recv()
+            share_copy(m, g, None, 1).wait_recv()
 
     def await_onward(g):
         for m in range(2):
-            for p in range(PIECES):
-                for t in far_steps:
-                    onward_copy(m, g, p, t).wait_recv()
+            for t in far_steps:
+                onward_copy(m, g, t).wait_recv()
 
     chunk = rows // 4
 
@@ -484,58 +514,70 @@
     smooth_keys(0)
     smooth_keys(1)
     for g in range(heads): send_far(V, g)
-    for copy in head_loads: copy.wait()
+    for g in range(heads): await_heads(g)
     hand_on(0)
+    attend(0, 2)
+    attend(1, 2)
     relay(S, 0)
-    await_halo(S, 0)
-    attend(0)
+    hand_on(1)
+    await_far(S, 0)
+    attend(0, 0)
     relay(S, 1)
-    hand_on(1)
-    await_halo(S, 1)
-    attend(1)
+    await_far(S, 1)
+    attend(1, 0)
+    hand_on(2)
+    await_near(S, 0)
+    attend(0, 1)
+    combine(0)
     relay(V, 0)
-    hand_on(2)
     near_grads(1, 0)
+    when(even, lambda: send_near_grads(1, 0))
+    far_grads(1, 0)
+    hand_on(3)
+    relay(V, 1)
+    when(odd, lambda: send_near_grads(1, 0))
+    await_near(S, 1)
+    attend(1, 1)
+    combine(1)
     near_grads(1, 1)
-    relay(V, 1)
-    send_near_grads(1, 0)
     send_near_grads(1, 1)
-    far_grads(1, 0)
     far_grads(1, 1)
-    hand_on(3)
-    await_halo(V, 0)
+    await_far(V, 0)
+    await_near(V, 0)
     differentiate(0)
     near_grads(0, 0)
     send_near_grads(0, 0)
     far_grads(0, 0)
     hand_on(4)
-    await_halo(V, 1)
+    await_far(V, 1)
+    await_near(V, 1)
     differentiate(1)
     near_grads(0, 1)
     send_near_grads(0, 1)
     join_grads(1, 0)
     far_grads(0, 1)
+    hand_on(5)
     own_grads(1, 0)
     join_grads(1, 1)
-    hand_on(5)
     own_grads(1, 1)
     own_grads(0, 0)
     own_grads(0, 1)
     join_grads(0, 0)
+    hand_on(6)
     finish(1, 0)
-    hand_on(6)
     query_grads(0)
+    hand_on(7)
+    finish(1, 1)
     join_grads(0, 1)
-    finish(1, 1)
+    hand_late(lambda copy: copy.start())
     finish(0, 0)
-    hand_on(7)
+    query_grads(1)
+    query_copy().start()
     for copy in own_copies: copy.wait()
     for copy in core_copies: copy.wait_recv()
     await_core(0)
     product((0, 1), 0, True, False)
     finish(0, 1)
-    query_grads(1)
-    query_copy().start()
     for m in (1, 0): pass_on(m, 0)
     await_core(1)
     product((0, 1), 1, False, False)
@@ -552,20 +594,19 @@
     when(b + 1 < n, lambda: near_sum().wait_send())
     for g in range(heads):
         when(b + 2 < n, lambda: key_copy(g).wait_send())
-        for p in range(PIECES):
-            for kind in (V, S):
-                when(b + 2 < n, lambda: far_copy(kind, g, p).wait_send())
-                when(even | (b >= 2), lambda: near_copy(kind, g, p).wait_send())
-            for m in range(2):
-                when(odd | (b >= 2), lambda: grad_copy(m, g, OVER_Y, p, 1).wait_send())
-                when(b >= 2, lambda: grad_copy(m, g, OVER_Z, p, -2).wait_send())
-                for t in far_steps + [1]:
-                    share_copy(m, g, p, t).wait_send()
-                for t in far_steps:
-                    onward_copy(m, g, p, t).wait_send()
+    halo = value.at[:, 0:own]
+    when(b + 2 < n, lambda: along(halo, halo, h_send.at[FAR], h_recv.at[0, 0, 0, FAR], 2).wait_send())
+    when(even | (b >= 2), lambda: along(halo, halo, h_send.at[NEAR], h_recv.at[0, 0, 0, FAR], 2).wait_send())
+    for over, condition in ((OVER_Y, odd | (b >= 2)), (OVER_Z, b >= 2)):
+        ref = grad_out.at[:, :, over]
+        when(condition, lambda: along(ref, ref, g_send.at[over], g_recv.at[0, 0, 0, 0], 2).wait_send())
+    for t in range(1, nh):
+        across(scaled, scaled, s_send.at[t - 1], s_recv.at[0, 0, 0], 1).wait_send()
+    crossed = weights.at[pl.ds(2, nh - 2), :, pl.ds(0, half), :]
+    across(crossed, crossed, w_send.at[0], w_recv.at[0], 1).wait_send()
     for j in range(len(chunks)):
-        cross_copy(j).wait_send()
         hand(j, lambda copy: copy.wait_send())
+    hand_late(lambda copy: copy.wait_send())
     for copy in core_copies:
         copy.wait_send()
 
@@ -609,6 +650,8 @@
                 pltpu.VMEM((D, 3 * tokens), BF16),
                 pltpu.VMEM((heads, 3 * tokens, group * tokens), BF16),
                 pltpu.VMEM((heads, 3 * tokens, group * tokens), BF16),
+                pltpu.VMEM((heads, 3, 2, group * tokens), F32),
+                pltpu.VMEM((heads, 3, group * tokens, D), BF16),
                 pltpu.VMEM((2, heads, tokens, D), F32),
                 pltpu.VMEM((2, heads, tokens, D), F32),
                 pltpu.VMEM((2, heads, 2, tokens, D), BF16),
@@ -620,14 +663,13 @@
                 pltpu.VMEM(q.shape, BF16),
                 pltpu.VMEM((rows, tokens), BF16),
                 dma((5,)),
-                dma((4,)), dma((heads, 2, group * tiles)), dma((2,)),
+                dma((4,)), dma((heads, 2)), dma((2,)),
                 dma((heads,)), dma((heads,)), dma((1,)), dma((1,)),
-                dma((2, heads, PIECES, 2)), dma((2, heads, PIECES, 2)),
-                dma((n_chunks,)), dma((n_chunks,)),
-                dma((n_chunks,)), dma((n_chunks,)), dma((n_chunks,)), dma((n_chunks,)),
+                dma((2,)), dma((2, heads, PIECES, 2)),
+                dma((1,)), dma((n_chunks,)), dma((n_chunks, 2)), dma((n_chunks,)),
                 dma((2,)), dma((2,)),
-                dma((2, heads, 2, PIECES)), dma((2, heads, 2, PIECES)),
-                dma((nh - 1, 2, heads, PIECES)), dma((nh - 1, 2, heads, PIECES)),
+                dma((2,)), dma((2, heads, 2, PIECES)),
+                dma((nh - 1,)), dma((nh - 1, 2, heads)),
             ],
             compiler_params=pltpu.CompilerParams(
                 collective_id=0, has_side_effects=True, vmem_limit_bytes=48 * 2**20

time: 58.9 us -> 55 us (0.934)
  the two profiles are of different devices: /device:TPU:0 before, /device:TPU:5 now
where the time goes in v2:
time: 55 us; the launch traced here: 54.9 us
  Pallas kernels  52.3 us (95%)
  local copies, waits for them, and re-layouts  1.87 us (3%)
  between operations  0.64 us (1%)
    pallas_call x1, Pallas kernels, local(): pl.pallas_call(functools.partial(kernel, n, nh), out_shape=(pltpu.VMEM(q....  52.3 us
    unnamed x2, local copies, waits for them, and re-layouts  1.87 us

profile of v2, /device:TPU:5, one launch (start us, length us, event | category | flops | bytes accessed | tf_op | source)
XLA Modules:
  0.0 54.9 jit_solution(15734595382860448147)
XLA Ops:
  0.6 52.3 %shard_map.95 = (bf16[512,512]{1,0:T(8,128)(2,1)S(1)}, bf16[1344,512]{1,0:T(8,128)(2,1)S(1)}) custom-call(bf16[512,512]{1,0:T(8,128)(2,1)} %q_ref.1, bf16[512,256]{1,0:T(8,128)(2,1)} %k_ref.1, bf16[512,256]{1,0:T(8,128)(2,1)} %v_ref.1, bf16[512,512]{1,0:T(8,128)(2,1)} %do_ref.1, s32[2,4]{1,0:T(2,128)} %bitcast.2, s32[2,4]{1,0:T(2,128)} %bitcast.3, ...), custom_call_target="tpu_custom_call" | custom-call | tf_op jit(solution)/shard_map/pallas_call | solution.py:628
  53.0 0.8 %copy.12 = bf16[512,512]{1,0:T(8,128)(2,1)} copy(bf16[512,512]{1,0:T(8,128)(2,1)S(1)} %get-tuple-element.2) | data formatting | bytes 1048576
  53.8 1.1 %copy.13 = bf16[1344,512]{1,0:T(8,128)(2,1)} copy(bf16[1344,512]{1,0:T(8,128)(2,1)S(1)} %get-tuple-element.3) | data formatting | bytes 2752512

commit v3 on v2

--- a/solution.py
+++ b/solution.py
@@ -47,7 +47,7 @@
     k_in, v_in, ke_in, ve_in, q_all, do_all, key_true, raw_far, own_sum, total_own, total_near, smooth, value, smooth_t,
     shares_all, score_all, stats, do_part, far_grad, own_grad, grad_out, grad_in, scaled, gathered, weights, acc,
     dq_ref, out_ref, out_sem, in_sem, qd_sem, w_own, kf_send, kf_recv, t_send, t_recv, h_send, h_recv,
-    w_send, w_recv, f_send, f_recv, c_send, c_recv, g_send, g_recv, s_send, s_recv,
+    w_send, w_recv, f_send, f_recv, thin_send, thin_recv, c_send, c_recv, g_send, g_recv, s_send, s_recv,
 ):
     tokens = k_ref.shape[0]
     heads = k_ref.shape[1] // D
@@ -127,11 +127,13 @@
 
     half = rows // 2
     part = half // 2
-    chunks = [(t, m, q) for q in range(2) for t in crossing for m in range(2)]
-    by_down = range(0, len(chunks) // 2)
-    by_up = range(len(chunks) // 2, len(chunks) * 3 // 4)
-    late = len(chunks) - 2
+    chunks = [(t, m, q) for t in crossing for m in range(2) for q in range(2)]
+    thin_t, thin_m = chunks[-1][:2]
+    chunks = chunks[:-2]
     w_refs = (wk_ref, wv_ref)
+    z = lax.div(b, 2)
+    upper = lax.rem(z, 2)
+    mine = lax.rem(lax.div(lax.rem(z, 4) + 1, 2), 2)
     row_0 = b < 2
     row_1 = (b >= 2) & (b < 4)
     top = b + 2 >= n
@@ -140,51 +142,78 @@
     def held(t, m, q, side):
         return weights.at[t, m, pl.ds(side * half + q * part, part), :]
 
-    def cross_copy(j):
-        t, m, q = chunks[j]
+    def cross(t, m, q, j):
         return across(
             w_refs[m].at[pl.ds(partner(h, t) * rows + colour * half + q * part, part), :],
-            held(t, m, q, colour), w_send.at[0], w_recv.at[j], t,
+            held(t, m, q, colour), w_send.at[j], w_recv.at[j], t,
         )
 
-    def down_copy(j, side):
-        ref = held(*chunks[j], side)
-        return along(ref, ref, f_send.at[j, 0], f_recv.at[j], -2)
-
-    def up_copy(j):
-        ref = held(*chunks[j], colour)
-        return along(ref, ref, f_send.at[j, 1], f_recv.at[j], 2)
-
-    def side_copy(j):
-        ref = held(*chunks[j], colour)
+    def cross_copy(j):
+        return cross(*chunks[j], j)
+
+    def cross_thin():
+        return cross(thin_t, thin_m, mine, len(chunks))
+
+    def hand_copy(ref, step, sent, received):
+        if step:
+            return along(ref, ref, sent, received, step)
         return pltpu.make_async_remote_copy(
-            src_ref=ref, dst_ref=ref, send_sem=f_send.at[j, 0], recv_sem=f_recv.at[j],
+            src_ref=ref, dst_ref=ref, send_sem=sent, recv_sem=received,
             device_id={"seq": partner(b, 1)}, device_id_type=MESH,
         )
 
+    def chunk_copy(j, step, which):
+        return hand_copy(held(*chunks[j], colour), step, f_send.at[j, which], f_recv.at[j])
+
     def hand(j, action):
-        if j in by_down:
-            when(b >= 4, lambda: action(down_copy(j, colour)))
-            when(below_top, lambda: action(up_copy(j)))
-            when(row_0, lambda: action(side_copy(j)))
-        elif j in by_up:
-            when(b + 2 < n, lambda: action(up_copy(j)))
-            if j == by_up[0]:
-                when(row_1, lambda: action(down_copy(j, colour)))
-            else:
-                when(row_0, lambda: action(side_copy(j)))
-        elif j == late:
-            when(b >= 2, lambda: action(side_copy(j)))
+        if j < 2:
+            when(b >= 2, lambda: action(chunk_copy(j, -2, 0)))
+            if j > 0:
+                when(below_top, lambda: action(chunk_copy(j, 2, 1)))
         else:
-            action(side_copy(j))
-
-    def hand_late(action):
-        ref = held(*chunks[late], colour)
-        when(row_1, lambda: action(along(ref, ref, f_send.at[late, 1], f_recv.at[late], -2)))
+            when(b + 2 < n, lambda: action(chunk_copy(j, 2, 1)))
+            if j != 3:
+                when(row_0, lambda: action(chunk_copy(j, 0, 0)))
 
     def hand_on(j):
         cross_copy(j).wait_recv()
         hand(j, lambda copy: copy.start())
+
+    def hand_top(action):
+        when(top, lambda: action(chunk_copy(0, 0, 1)))
+
+    def hand_bottom(action):
+        when(row_1, lambda: action(chunk_copy(3, -2, 0)))
+
+    def thin_copy(which, step, sent, received, side=colour):
+        return hand_copy(held(thin_t, thin_m, which, side), step, sent, received)
+
+    def thin_up():
+        return thin_copy(mine, 2, thin_send.at[0], thin_recv.at[0])
+
+    def thin_down():
+        return thin_copy(mine, -2, thin_send.at[0], thin_recv.at[0])
+
+    def thin_side(which, at, side=colour):
+        return thin_copy(which, 0, thin_send.at[at], thin_recv.at[at], side)
+
+    def hand_thin():
+        cross_thin().wait_recv()
+        thin_side(mine, 1).start()
+        when(upper == 1, lambda: thin_down().start())
+
+    def raise_thin():
+        when(upper == 0, lambda: thin_up().start())
+
+    def share_thin():
+        thin_copy(1 - mine, 2, thin_send.at[0], thin_recv.at[0], 1 - colour).wait_recv()
+        thin_side(1 - mine, 2, 1 - colour).start()
+
+    def await_weights():
+        for j in range(len(chunks)):
+            hand_copy(held(*chunks[j], 1 - colour), 0, f_send.at[j, 0], f_recv.at[j]).wait_recv()
+        thin_side(mine, 1, 1 - colour).wait_recv()
+        thin_side(1 - mine, 2).wait_recv()
 
     core_copies = [
         across(ref.at[pl.ds(partner(h, 1) * rows, rows), :], weights.at[1, m], c_send.at[m], c_recv.at[m], 1)
@@ -500,6 +529,7 @@
 
     pl.semaphore_wait(barrier, greeted)
     for copy in loads: copy.wait()
+    cross_thin().start()
     for j in range(len(chunks)): cross_copy(j).start()
     for g in range(heads): true_keys(g)
     sum_keys()
@@ -512,20 +542,22 @@
     for g in range(heads): running_keys(g)
     when(b >= 1, lambda: near_sum().wait_recv())
     smooth_keys(0)
+    hand_thin()
     smooth_keys(1)
     for g in range(heads): send_far(V, g)
+    raise_thin()
     for g in range(heads): await_heads(g)
-    hand_on(0)
     attend(0, 2)
     attend(1, 2)
     relay(S, 0)
-    hand_on(1)
+    hand_on(0)
     await_far(S, 0)
     attend(0, 0)
     relay(S, 1)
     await_far(S, 1)
     attend(1, 0)
-    hand_on(2)
+    hand_on(1)
+    when(row_0, share_thin)
     await_near(S, 0)
     attend(0, 1)
     combine(0)
@@ -533,43 +565,42 @@
     near_grads(1, 0)
     when(even, lambda: send_near_grads(1, 0))
     far_grads(1, 0)
-    hand_on(3)
     relay(V, 1)
     when(odd, lambda: send_near_grads(1, 0))
     await_near(S, 1)
     attend(1, 1)
+    hand_on(2)
     combine(1)
     near_grads(1, 1)
     send_near_grads(1, 1)
     far_grads(1, 1)
     await_far(V, 0)
     await_near(V, 0)
+    join_grads(1, 0)
     differentiate(0)
     near_grads(0, 0)
     send_near_grads(0, 0)
+    hand_on(3)
     far_grads(0, 0)
-    hand_on(4)
     await_far(V, 1)
     await_near(V, 1)
+    join_grads(1, 1)
     differentiate(1)
     near_grads(0, 1)
     send_near_grads(0, 1)
-    join_grads(1, 0)
+    hand_on(4)
+    when(b >= 2, share_thin)
+    hand_top(lambda copy: copy.start())
     far_grads(0, 1)
+    for m in (1, 0): own_grads(m, 0)
+    join_grads(0, 0)
+    finish(1, 0)
+    for m in (1, 0): own_grads(m, 1)
     hand_on(5)
-    own_grads(1, 0)
-    join_grads(1, 1)
-    own_grads(1, 1)
-    own_grads(0, 0)
-    own_grads(0, 1)
-    join_grads(0, 0)
-    hand_on(6)
-    finish(1, 0)
+    join_grads(0, 1)
+    hand_bottom(lambda copy: copy.start())
+    finish(1, 1)
     query_grads(0)
-    hand_on(7)
-    finish(1, 1)
-    join_grads(0, 1)
-    hand_late(lambda copy: copy.start())
     finish(0, 0)
     query_grads(1)
     query_copy().start()
@@ -578,10 +609,10 @@
     await_core(0)
     product((0, 1), 0, True, False)
     finish(0, 1)
-    for m in (1, 0): pass_on(m, 0)
     await_core(1)
     product((0, 1), 1, False, False)
-    for j in range(len(chunks)): down_copy(j, 1 - colour).wait_recv()
+    for m in (1, 0): pass_on(m, 0)
+    await_weights()
     await_onward(0)
     product(crossing, 0, False, False)
     for m in (1, 0): pass_on(m, 1)
@@ -602,18 +633,22 @@
         when(condition, lambda: along(ref, ref, g_send.at[over], g_recv.at[0, 0, 0, 0], 2).wait_send())
     for t in range(1, nh):
         across(scaled, scaled, s_send.at[t - 1], s_recv.at[0, 0, 0], 1).wait_send()
-    crossed = weights.at[pl.ds(2, nh - 2), :, pl.ds(0, half), :]
-    across(crossed, crossed, w_send.at[0], w_recv.at[0], 1).wait_send()
+    cross_thin().wait_send()
+    thin_up().wait_send()
+    thin_side(mine, 1).wait_send()
+    thin_side(1 - mine, 2, 1 - colour).wait_send()
     for j in range(len(chunks)):
+        cross_copy(j).wait_send()
         hand(j, lambda copy: copy.wait_send())
-    hand_late(lambda copy: copy.wait_send())
+    hand_top(lambda copy: copy.wait_send())
+    hand_bottom(lambda copy: copy.wait_send())
     for copy in core_copies:
         copy.wait_send()
 
 
 def solution(mesh):
     n, nh = mesh.shape["seq"], mesh.shape["head"]
-    assert n % 2 == 0 and n >= 4
+    assert n % 8 == 0 and nh >= 4
 
     def local(q, k, v, do, ke, ve, wk, wv):
         tokens, width = k.shape
@@ -666,7 +701,7 @@
                 dma((4,)), dma((heads, 2)), dma((2,)),
                 dma((heads,)), dma((heads,)), dma((1,)), dma((1,)),
                 dma((2,)), dma((2, heads, PIECES, 2)),
-                dma((1,)), dma((n_chunks,)), dma((n_chunks, 2)), dma((n_chunks,)),
+                dma((n_chunks - 1,)), dma((n_chunks - 1,)), dma((n_chunks - 2, 2)), dma((n_chunks - 2,)), dma((3,)), dma((3,)),
                 dma((2,)), dma((2,)),
                 dma((2,)), dma((2, heads, 2, PIECES)),
                 dma((nh - 1,)), dma((nh - 1, 2, heads)),

time: 55 us -> 52.9 us (0.962)
  the two profiles are of different devices: /device:TPU:5 before, /device:TPU:25 now
where the time goes in v3:
time: 52.9 us; the launch traced here: 52.8 us
  Pallas kernels  50.2 us (95%)
  local copies, waits for them, and re-layouts  1.87 us (4%)
  between operations  0.64 us (1%)
    pallas_call x1, Pallas kernels, local(): pl.pallas_call(functools.partial(kernel, n, nh), out_shape=(pltpu.VMEM(q....  50.2 us
    unnamed x2, local copies, waits for them, and re-layouts  1.87 us

profile of v3, /device:TPU:25, one launch (start us, length us, event | category | flops | bytes accessed | tf_op | source)
XLA Modules:
  0.0 52.8 jit_solution(8376929546388276015)
XLA Ops:
  0.6 50.2 %shard_map.95 = (bf16[512,512]{1,0:T(8,128)(2,1)S(1)}, bf16[1344,512]{1,0:T(8,128)(2,1)S(1)}) custom-call(bf16[512,512]{1,0:T(8,128)(2,1)} %q_ref.1, bf16[512,256]{1,0:T(8,128)(2,1)} %k_ref.1, bf16[512,256]{1,0:T(8,128)(2,1)} %v_ref.1, bf16[512,512]{1,0:T(8,128)(2,1)} %do_ref.1, s32[2,4]{1,0:T(2,128)} %bitcast.2, s32[2,4]{1,0:T(2,128)} %bitcast.3, ...), custom_call_target="tpu_custom_call" | custom-call | tf_op jit(solution)/shard_map/pallas_call | solution.py:663
  50.9 0.8 %copy.12 = bf16[512,512]{1,0:T(8,128)(2,1)} copy(bf16[512,512]{1,0:T(8,128)(2,1)S(1)} %get-tuple-element.2) | data formatting | bytes 1048576
  51.7 1.1 %copy.13 = bf16[1344,512]{1,0:T(8,128)(2,1)} copy(bf16[1344,512]{1,0:T(8,128)(2,1)S(1)} %get-tuple-element.3) | data formatting | bytes 2752512

commit v4 on v3

--- a/solution.py
+++ b/solution.py
@@ -20,6 +20,7 @@
 TILE = SCALE_BLOCK
 SPAN = ATTEND_WINDOW + TILE
 PIECES = 2
+CHUNKS = 4
 V, S = 0, 1
 FAR, NEAR = 0, 1
 OVER_Y, OVER_Z = 0, 1
@@ -43,10 +44,10 @@
 
 
 def kernel(
-    n, nh, q_ref, k_ref, v_ref, do_ref, ke_ref, ve_ref, wk_ref, wv_ref, dq_out, grad_rows,
+    n, nh, q_ref, k_ref, v_ref, do_ref, ke_ref, ve_ref, wk_ref, wv_ref, dq_ref, gathered, weights, acc,
     k_in, v_in, ke_in, ve_in, q_all, do_all, key_true, raw_far, own_sum, total_own, total_near, smooth, value, smooth_t,
-    shares_all, score_all, stats, do_part, far_grad, own_grad, grad_out, grad_in, scaled, gathered, weights, acc,
-    dq_ref, out_ref, out_sem, in_sem, qd_sem, w_own, kf_send, kf_recv, t_send, t_recv, h_send, h_recv,
+    shares_all, score_all, stats, do_part, far_grad, own_grad, grad_out, grad_in, scaled,
+    in_sem, qd_sem, w_own, kf_send, kf_recv, t_send, t_recv, h_send, h_recv,
     w_send, w_recv, f_send, f_recv, thin_send, thin_recv, c_send, c_recv, g_send, g_recv, s_send, s_recv,
 ):
     tokens = k_ref.shape[0]
@@ -54,7 +55,7 @@
     group = q_ref.shape[1] // (heads * D)
     width = group * TILE
     tiles = tokens // TILE
-    rows = grad_rows.shape[0]
+    rows = acc.shape[0]
     own = 2 * tokens
     scale = QUERY_SCALE ** (-0.5)
     b = lax.axis_index("seq")
@@ -213,6 +214,8 @@
         for j in range(len(chunks)):
             hand_copy(held(*chunks[j], 1 - colour), 0, f_send.at[j, 0], f_recv.at[j]).wait_recv()
         thin_side(mine, 1, 1 - colour).wait_recv()
+
+    def await_thin():
         thin_side(1 - mine, 2).wait_recv()
 
     core_copies = [
@@ -497,17 +500,11 @@
             for t in far_steps:
                 onward_copy(m, g, t).wait_recv()
 
-    chunk = rows // 4
-
-    def row_copy(c):
-        at = pl.ds(pl.multiple_of(c * chunk, 16), chunk)
-        return pltpu.make_async_copy(out_ref.at[at, :], grad_rows.at[at, :], out_sem.at[c])
-
-    def query_copy():
-        return pltpu.make_async_copy(dq_ref, dq_out, out_sem.at[4])
-
-    def product(ts, g, fresh, last):
-        def one_chunk(c, carry):
+    chunk = rows // CHUNKS
+
+    def product(ts, g, fresh, base=0, count=CHUNKS):
+        def one_chunk(k, carry):
+            c = base + k
             at = pl.ds(pl.multiple_of(c * chunk, 16), chunk)
             total = None if fresh else acc[at, :]
             for t in ts:
@@ -518,14 +515,10 @@
                     right = jnp.concatenate([gathered[t - 1, 0, g], gathered[t - 1, 1, g]], 1)
                 term = contract_last(left, right)
                 total = term if total is None else total + term
-            if last:
-                out_ref[at, :] = total.astype(BF16)
-                row_copy(c).start()
-            else:
-                acc[at, :] = total
+            acc[at, :] = total
             return carry
 
-        lax.fori_loop(0, 4, one_chunk, 0)
+        lax.fori_loop(0, count, one_chunk, 0)
 
     pl.semaphore_wait(barrier, greeted)
     for copy in loads: copy.wait()
@@ -553,11 +546,11 @@
     hand_on(0)
     await_far(S, 0)
     attend(0, 0)
+    when(row_0, share_thin)
     relay(S, 1)
     await_far(S, 1)
     attend(1, 0)
     hand_on(1)
-    when(row_0, share_thin)
     await_near(S, 0)
     attend(0, 1)
     combine(0)
@@ -581,7 +574,6 @@
     near_grads(0, 0)
     send_near_grads(0, 0)
     hand_on(3)
-    far_grads(0, 0)
     await_far(V, 1)
     await_near(V, 1)
     join_grads(1, 1)
@@ -591,6 +583,7 @@
     hand_on(4)
     when(b >= 2, share_thin)
     hand_top(lambda copy: copy.start())
+    far_grads(0, 0)
     far_grads(0, 1)
     for m in (1, 0): own_grads(m, 0)
     join_grads(0, 0)
@@ -603,25 +596,22 @@
     query_grads(0)
     finish(0, 0)
     query_grads(1)
-    query_copy().start()
     for copy in own_copies: copy.wait()
     for copy in core_copies: copy.wait_recv()
     await_core(0)
-    product((0, 1), 0, True, False)
+    product((0, 1), 0, True)
     finish(0, 1)
     await_core(1)
-    product((0, 1), 1, False, False)
+    product((0, 1), 1, False)
     for m in (1, 0): pass_on(m, 0)
+    await_onward(0)
+    await_thin()
+    product(crossing, 0, False, 2 * colour, 2)
+    for m in (1, 0): pass_on(m, 1)
     await_weights()
-    await_onward(0)
-    product(crossing, 0, False, False)
-    for m in (1, 0): pass_on(m, 1)
+    product(crossing, 0, False, 2 - 2 * colour, 2)
     await_onward(1)
-    product(crossing, 1, False, True)
-
-    query_copy().wait()
-    for c in range(4):
-        row_copy(c).wait()
+
     when(b + 1 < n, lambda: near_sum().wait_send())
     for g in range(heads):
         when(b + 2 < n, lambda: key_copy(g).wait_send())
@@ -646,6 +636,29 @@
         copy.wait_send()
 
 
+def last_product(nh, heads, dq_ref, gathered, weights, acc, dq_out, grad_rows, out_ref, sem):
+    rows = acc.shape[0]
+    chunk = rows // CHUNKS
+    g = heads - 1
+    cols = slice(g * D, (g + 1) * D)
+    query_copy = pltpu.make_async_copy(dq_ref, dq_out, sem.at[CHUNKS])
+    query_copy.start()
+    copies = []
+    for c in range(CHUNKS):
+        at = slice(c * chunk, (c + 1) * chunk)
+        total = acc[at, :]
+        for t in range(2, nh):
+            left = jnp.concatenate([weights[t, 0, at, cols], weights[t, 1, at, cols]], 1)
+            right = jnp.concatenate([gathered[t - 1, 0, g], gathered[t - 1, 1, g]], 1)
+            total = total + contract_last(left, right)
+        out_ref[at, :] = total.astype(BF16)
+        copies.append(pltpu.make_async_copy(out_ref.at[at, :], grad_rows.at[at, :], sem.at[c]))
+        copies[-1].start()
+    query_copy.wait()
+    for copy in copies:
+        copy.wait()
+
+
 def solution(mesh):
     n, nh = mesh.shape["seq"], mesh.shape["head"]
     assert n % 8 == 0 and nh >= 4
@@ -660,14 +673,17 @@
         n_chunks = 4 * (nh - 2)
         hbm = pl.BlockSpec(memory_space=pltpu.HBM)
         dma = pltpu.SemaphoreType.DMA
-        return pl.pallas_call(
+        vmem = pl.BlockSpec(memory_space=pltpu.VMEM)
+        parts = pl.pallas_call(
             functools.partial(kernel, n, nh),
             out_shape=(
                 pltpu.VMEM(q.shape, BF16),
-                pltpu.VMEM((rows, tokens), BF16),
+                pltpu.VMEM((nh - 1, 2, heads, tokens, D), BF16),
+                pltpu.VMEM((nh, 2, rows, width), BF16),
+                pltpu.VMEM((rows, tokens), F32),
             ),
             in_specs=[hbm] * 8,
-            out_specs=(pl.BlockSpec(memory_space=pl.ANY),) * 2,
+            out_specs=(vmem,) * 4,
             scratch_shapes=[
                 pltpu.VMEM((tokens, width), BF16),
                 pltpu.VMEM((tokens, width), BF16),
@@ -692,12 +708,6 @@
                 pltpu.VMEM((2, heads, 2, tokens, D), BF16),
                 pltpu.VMEM((2, heads, 2, tokens, D), BF16),
                 pltpu.VMEM((2, heads, tokens, D), BF16),
-                pltpu.VMEM((nh - 1, 2, heads, tokens, D), BF16),
-                pltpu.VMEM((nh, 2, rows, width), BF16),
-                pltpu.VMEM((rows, tokens), F32),
-                pltpu.VMEM(q.shape, BF16),
-                pltpu.VMEM((rows, tokens), BF16),
-                dma((5,)),
                 dma((4,)), dma((heads, 2)), dma((2,)),
                 dma((heads,)), dma((heads,)), dma((1,)), dma((1,)),
                 dma((2,)), dma((2, heads, PIECES, 2)),
@@ -710,6 +720,17 @@
                 collective_id=0, has_side_effects=True, vmem_limit_bytes=48 * 2**20
             ),
         )(*[pltpu.with_memory_space_constraint(x, pltpu.HBM) for x in (q, k, v, do, ke.T, ve.T, wk, wv)])
+        return pl.pallas_call(
+            functools.partial(last_product, nh, heads),
+            out_shape=(
+                jax.ShapeDtypeStruct(q.shape, BF16),
+                jax.ShapeDtypeStruct((rows, tokens), BF16),
+            ),
+            in_specs=[vmem] * 4,
+            out_specs=(pl.BlockSpec(memory_space=pl.ANY),) * 2,
+            scratch_shapes=[pltpu.VMEM((rows, tokens), BF16), dma((CHUNKS + 1,))],
+            compiler_params=pltpu.CompilerParams(vmem_limit_bytes=24 * 2**20),
+        )(*[pltpu.with_memory_space_constraint(x, pltpu.VMEM) for x in parts])
 
     in_specs = (P("seq", "head"),) * 6 + (P(None, "head"),) * 2
     out_specs = (P("seq", "head"), P("head", "seq"))

time: 52.9 us -> 48.4 us (0.915)
  the two profiles are of different devices: /device:TPU:25 before, /device:TPU:0 now
where the time goes in v4:
time: 48.4 us; the launch traced here: 48.3 us
  Pallas kernels  47.5 us (98%)
  between operations  0.8 us (2%)
    pallas_call x1, Pallas kernels, local(): pl.pallas_call(functools.partial(kernel, n, nh), out_shape=(pltpu.VMEM(q....  45.8 us
    pallas_call x1, Pallas kernels, local(): pl.pallas_call(functools.partial(last_product, nh, heads), out_shape=(jax...  1.69 us

profile of v4, /device:TPU:0, one launch (start us, length us, event | category | flops | bytes accessed | tf_op | source)
XLA Modules:
  0.0 48.3 jit_solution(8762920677483224335)
XLA Ops:
  0.6 45.8 %shard_map.95 = (bf16[512,512]{1,0:T(8,128)(2,1)S(1)}, bf16[3,2,2,512,128]{4,3,2,1,0:T(8,128)(2,1)S(1)}, bf16[4,2,1344,256]{3,2,1,0:T(8,128)(2,1)S(1)}, f32[1344,512]{1,0:T(8,128)S(1)}) custom-call(bf16[512,512]{1,0:T(8,128)(2,1)} %q_ref.1, bf16[512,256]{1,0:T(8,128)(2,1)} %k_ref.1, bf16[512,256]{1,0:T(8,128)(2,1)} %v_ref.1, bf16[512,512]{1,0:T(8,128)(2,1)} %do_ref.1, ...), custom_call_target="tpu_custom_call" | custom-call | tf_op jit(solution)/shard_map/pallas_call | solution.py:677
  46.4 1.7 %shard_map.96 = (bf16[512,512]{1,0:T(8,128)(2,1)}, bf16[1344,512]{1,0:T(8,128)(2,1)}) custom-call(bf16[512,512]{1,0:T(8,128)(2,1)S(1)} %get-tuple-element.6.dq_ref, bf16[3,2,2,512,128]{4,3,2,1,0:T(8,128)(2,1)S(1)} %get-tuple-element.7.gathered, bf16[4,2,1344,256]{3,2,1,0:T(8,128)(2,1)S(1)} %get-tuple-element.8.weights, f32[1344,512]{1,0:T(8,128)S(1)} %get-tuple-element.9.acc), custom_call_target="tpu_custom_call" | custom-call | tf_op jit(solution)/shard_map/pallas_call | solution.py:723

commit v5 on v4

--- a/solution.py
+++ b/solution.py
@@ -20,7 +20,8 @@
 TILE = SCALE_BLOCK
 SPAN = ATTEND_WINDOW + TILE
 PIECES = 2
-CHUNKS = 4
+CHUNKS = 2
+LAST_CHUNKS = 4
 V, S = 0, 1
 FAR, NEAR = 0, 1
 OVER_Y, OVER_Z = 0, 1
@@ -302,7 +303,6 @@
             total_own[:, cols(g)] = jnp.broadcast_to(
                 jnp.sum(key_true[g].astype(F32), axis=0, keepdims=True), (8, D)
             )
-        when(b + 1 < n, lambda: near_sum().start())
 
     def clear():
         @pl.when(b < 1)
@@ -520,16 +520,16 @@
 
         lax.fori_loop(0, count, one_chunk, 0)
 
+    for copy in loads: copy.wait()
+    for g in range(heads): true_keys(g)
+    sum_keys()
+    for g in range(heads): true_values(g)
     pl.semaphore_wait(barrier, greeted)
-    for copy in loads: copy.wait()
+    when(b + 1 < n, lambda: near_sum().start())
     cross_thin().start()
     for j in range(len(chunks)): cross_copy(j).start()
-    for g in range(heads): true_keys(g)
-    sum_keys()
     for g in range(heads): when(b + 2 < n, lambda: key_copy(g).start())
-    for g in range(heads):
-        true_values(g)
-        send_near(V, g)
+    for g in range(heads): send_near(V, g)
     for copy in core_copies + own_copies: copy.start()
     clear()
     for g in range(heads): running_keys(g)
@@ -590,9 +590,9 @@
     finish(1, 0)
     for m in (1, 0): own_grads(m, 1)
     hand_on(5)
+    finish(1, 1)
     join_grads(0, 1)
     hand_bottom(lambda copy: copy.start())
-    finish(1, 1)
     query_grads(0)
     finish(0, 0)
     query_grads(1)
@@ -606,10 +606,10 @@
     for m in (1, 0): pass_on(m, 0)
     await_onward(0)
     await_thin()
-    product(crossing, 0, False, 2 * colour, 2)
+    product(crossing, 0, False, colour, 1)
     for m in (1, 0): pass_on(m, 1)
     await_weights()
-    product(crossing, 0, False, 2 - 2 * colour, 2)
+    product(crossing, 0, False, 1 - colour, 1)
     await_onward(1)
 
     when(b + 1 < n, lambda: near_sum().wait_send())
@@ -638,13 +638,13 @@
 
 def last_product(nh, heads, dq_ref, gathered, weights, acc, dq_out, grad_rows, out_ref, sem):
     rows = acc.shape[0]
-    chunk = rows // CHUNKS
+    chunk = rows // LAST_CHUNKS
     g = heads - 1
     cols = slice(g * D, (g + 1) * D)
-    query_copy = pltpu.make_async_copy(dq_ref, dq_out, sem.at[CHUNKS])
+    query_copy = pltpu.make_async_copy(dq_ref, dq_out, sem.at[LAST_CHUNKS])
     query_copy.start()
     copies = []
-    for c in range(CHUNKS):
+    for c in range(LAST_CHUNKS):
         at = slice(c * chunk, (c + 1) * chunk)
         total = acc[at, :]
         for t in range(2, nh):
@@ -728,7 +728,7 @@
             ),
             in_specs=[vmem] * 4,
             out_specs=(pl.BlockSpec(memory_space=pl.ANY),) * 2,
-            scratch_shapes=[pltpu.VMEM((rows, tokens), BF16), dma((CHUNKS + 1,))],
+            scratch_shapes=[pltpu.VMEM((rows, tokens), BF16), dma((LAST_CHUNKS + 1,))],
             compiler_params=pltpu.CompilerParams(vmem_limit_bytes=24 * 2**20),
         )(*[pltpu.with_memory_space_constraint(x, pltpu.VMEM) for x in parts])
 

time: 48.4 us -> 48 us (level)
  Pallas kernels: 47.5 us -> 46.9 us
    pallas_call x1, Pallas kernels: 45.8 us -> 45.2 us  [local(): pl.pallas_call(functools.partial(kernel, n, nh), out_shape=(pltpu.VMEM(q....]
where the time goes in v5:
time: 48 us; the launch traced here: 47.7 us
  Pallas kernels  46.9 us (98%)
  between operations  0.8 us (2%)
    pallas_call x1, Pallas kernels, local(): pl.pallas_call(functools.partial(kernel, n, nh), out_shape=(pltpu.VMEM(q....  45.2 us
    pallas_call x1, Pallas kernels, local(): pl.pallas_call(functools.partial(last_product, nh, heads), out_shape=(jax...  1.69 us

profile of v5, /device:TPU:0, one launch (start us, length us, event | category | flops | bytes accessed | tf_op | source)
XLA Modules:
  0.0 47.7 jit_solution(3057996101112924593)
XLA Ops:
  0.6 45.2 %shard_map.95 = (bf16[512,512]{1,0:T(8,128)(2,1)S(1)}, bf16[3,2,2,512,128]{4,3,2,1,0:T(8,128)(2,1)S(1)}, bf16[4,2,1344,256]{3,2,1,0:T(8,128)(2,1)S(1)}, f32[1344,512]{1,0:T(8,128)S(1)}) custom-call(bf16[512,512]{1,0:T(8,128)(2,1)} %q_ref.1, bf16[512,256]{1,0:T(8,128)(2,1)} %k_ref.1, bf16[512,256]{1,0:T(8,128)(2,1)} %v_ref.1, bf16[512,512]{1,0:T(8,128)(2,1)} %do_ref.1, ...), custom_call_target="tpu_custom_call" | custom-call | tf_op jit(solution)/shard_map/pallas_call | solution.py:677
  45.8 1.7 %shard_map.96 = (bf16[512,512]{1,0:T(8,128)(2,1)}, bf16[1344,512]{1,0:T(8,128)(2,1)}) custom-call(bf16[512,512]{1,0:T(8,128)(2,1)S(1)} %get-tuple-element.6.dq_ref, bf16[3,2,2,512,128]{4,3,2,1,0:T(8,128)(2,1)S(1)} %get-tuple-element.7.gathered, bf16[4,2,1344,256]{3,2,1,0:T(8,128)(2,1)S(1)} %get-tuple-element.8.weights, f32[1344,512]{1,0:T(8,128)S(1)} %get-tuple-element.9.acc), custom_call_target="tpu_custom_call" | custom-call | tf_op jit(solution)/shard_map/pallas_call | solution.py:723

commit v6 on v5

--- a/solution.py
+++ b/solution.py
@@ -47,9 +47,9 @@
 def kernel(
     n, nh, q_ref, k_ref, v_ref, do_ref, ke_ref, ve_ref, wk_ref, wv_ref, dq_ref, gathered, weights, acc,
     k_in, v_in, ke_in, ve_in, q_all, do_all, key_true, raw_far, own_sum, total_own, total_near, smooth, value, smooth_t,
-    shares_all, score_all, stats, do_part, far_grad, own_grad, grad_out, grad_in, scaled,
+    shares_all, score_all, stats, do_part, early_grad, far_grad, own_grad, grad_out, grad_in, scaled,
     in_sem, qd_sem, w_own, kf_send, kf_recv, t_send, t_recv, h_send, h_recv,
-    w_send, w_recv, f_send, f_recv, thin_send, thin_recv, c_send, c_recv, g_send, g_recv, s_send, s_recv,
+    w_send, w_recv, f_send, f_recv, thin_send, thin_recv, c_send, c_recv, g_send, g_recv, s_send, s_recv, s_last,
 ):
     tokens = k_ref.shape[0]
     heads = k_ref.shape[1] // D
@@ -75,6 +75,20 @@
         pltpu.make_async_copy(ke_ref, ke_in, in_sem.at[2]),
         pltpu.make_async_copy(ve_ref, ve_in, in_sem.at[3]),
     ]
+    barrier = pltpu.get_barrier_semaphore()
+
+    def greet(step):
+        pl.semaphore_signal(
+            barrier, inc=1, device_id={"seq": lax.rem(b + n + step, n)}, device_id_type=MESH
+        )
+
+    for step in (1, 2):
+        pl.when(b + step < n)(lambda: greet(step))
+        pl.when(b >= step)(lambda: greet(-step))
+    for t in range(1, nh):
+        pl.semaphore_signal(barrier, inc=1, device_id={"head": partner(h, t)}, device_id_type=MESH)
+    greeted = nh - 1 + jnp.minimum(b, 2) + jnp.minimum(n - 1 - b, 2)
+
     for copy in loads:
         copy.start()
     head_loads = []
@@ -89,22 +103,7 @@
                             qd_sem.at[g, m],
                         )
                     )
-    for copy in head_loads:
-        copy.start()
-
-    barrier = pltpu.get_barrier_semaphore()
-
-    def greet(step):
-        pl.semaphore_signal(
-            barrier, inc=1, device_id={"seq": lax.rem(b + n + step, n)}, device_id_type=MESH
-        )
-
-    for step in (1, 2):
-        pl.when(b + step < n)(lambda: greet(step))
-        pl.when(b >= step)(lambda: greet(-step))
-    for t in range(1, nh):
-        pl.semaphore_signal(barrier, inc=1, device_id={"head": partner(h, t)}, device_id_type=MESH)
-    greeted = nh - 1 + jnp.minimum(b, 2) + jnp.minimum(n - 1 - b, 2)
+
 
     def when(condition, action):
         pl.when(condition)(action)
@@ -398,19 +397,32 @@
                     spread, do_all[g, at, :], preferred_element_type=F32
                 ).astype(BF16)
 
+    def local_of(part, i):
+        return slice(i * TILE, tokens) if part == 0 else slice(0, (i + 1) * TILE)
+
+    def differentiate_early(g):
+        for i in range(tiles):
+            lanes, row_dot = lanes_of(i), 0.0
+            for part in (0, 2):
+                at = keys_of(part, i)
+                share_grad = contract_last(value[g, at, :], do_part[g, part, lanes, :])
+                early_grad[g, part // 2, local_of(part, i), lanes] = share_grad
+                row_dot = row_dot + jnp.sum(shares_all[g, at, lanes].astype(F32) * share_grad, axis=0, keepdims=True)
+            stats[g, 0, 1:2, lanes] = row_dot
+
     def differentiate(g):
         for i in range(tiles):
             lanes = lanes_of(i)
-            row_dot, parts = 0.0, []
-            for part in range(3):
+            at = keys_of(1, i)
+            near_grad = contract_last(value[g, at, :], do_part[g, 1, lanes, :])
+            near_shares = shares_all[g, at, lanes].astype(F32)
+            row_dot = stats[g, 0, 1:2, lanes] + jnp.sum(near_shares * near_grad, axis=0, keepdims=True)
+            score_all[g, at, lanes] = (near_shares * (near_grad - row_dot * stats[g, 1, 0:1, lanes])).astype(BF16)
+            for part in (0, 2):
                 at = keys_of(part, i)
-                share_grad = contract_last(value[g, at, :], do_part[g, part, lanes, :])
-                shares = shares_all[g, at, lanes].astype(F32)
-                row_dot = row_dot + jnp.sum(shares * share_grad, axis=0, keepdims=True)
-                parts.append((at, shares, share_grad))
-            for part, (at, shares, share_grad) in enumerate(parts):
+                share_grad = early_grad[g, part // 2, local_of(part, i), lanes]
                 shift = row_dot * stats[g, part, 0:1, lanes]
-                score_all[g, at, lanes] = (shares * (share_grad - shift)).astype(BF16)
+                score_all[g, at, lanes] = (shares_all[g, at, lanes].astype(F32) * (share_grad - shift)).astype(BF16)
 
     def key_grads(m, g, part, at, lanes):
         if m == 0:
@@ -466,10 +478,17 @@
 
     def share_copy(m, g, p, t):
         at = (m, g) if p is None else (m, g, rows_of(p))
-        return across(scaled.at[at], gathered.at[(t - 1,) + at], s_send.at[t - 1], s_recv.at[t - 1, m, g], t)
-
-    def onward_copy(m, g, t):
-        return across(gathered.at[t - 1, m, g], gathered.at[t, m, g], s_send.at[t], s_recv.at[t, m, g], 1)
+        last = (m, g) == (0, heads - 1) and t > 1
+        received = s_last.at[t - 1, p] if last else s_recv.at[t - 1, m, g]
+        return across(scaled.at[at], gathered.at[(t - 1,) + at], s_send.at[t - 1], received, t)
+
+    def onward_copy(m, g, t, p=None):
+        at = (m, g) if p is None else (m, g, rows_of(p))
+        received = s_recv.at[t, m, g] if p is None else s_last.at[t, p]
+        return across(gathered.at[(t - 1,) + at], gathered.at[(t,) + at], s_send.at[t], received, 1)
+
+    def hops_of(m, g):
+        return range(PIECES) if (m, g) == (0, heads - 1) else (None,)
 
     far_steps = list(range(2, nh, 2))
 
@@ -488,37 +507,38 @@
 
     def pass_on(m, g):
         for t in far_steps:
-            share_copy(m, g, None, t).wait_recv()
-            onward_copy(m, g, t).start()
+            for p in hops_of(m, g):
+                share_copy(m, g, p, t).wait_recv()
+                onward_copy(m, g, t, p).start()
 
     def await_core(g):
         for m in range(2):
             share_copy(m, g, None, 1).wait_recv()
 
-    def await_onward(g):
-        for m in range(2):
-            for t in far_steps:
-                onward_copy(m, g, t).wait_recv()
+    def await_onward(m, g):
+        for t in far_steps:
+            for p in hops_of(m, g):
+                onward_copy(m, g, t, p).wait_recv()
 
     chunk = rows // CHUNKS
 
-    def product(ts, g, fresh, base=0, count=CHUNKS):
+    def product(terms, fresh, base=0, count=CHUNKS):
         def one_chunk(k, carry):
-            c = base + k
-            at = pl.ds(pl.multiple_of(c * chunk, 16), chunk)
-            total = None if fresh else acc[at, :]
-            for t in ts:
-                left = jnp.concatenate([weights[t, 0, at, cols(g)], weights[t, 1, at, cols(g)]], 1)
-                if t == 0:
-                    right = jnp.concatenate([scaled[0, g], scaled[1, g]], 1)
-                else:
-                    right = jnp.concatenate([gathered[t - 1, 0, g], gathered[t - 1, 1, g]], 1)
-                term = contract_last(left, right)
-                total = term if total is None else total + term
+            at = pl.ds(pl.multiple_of((base + k) * chunk, 16), chunk)
+            left = jnp.concatenate([weights[t, m, at, cols(g)] for t, m, g in terms], 1)
+            right = [scaled[m, g] if t == 0 else gathered[t - 1, m, g] for t, m, g in terms]
+            total = contract_last(left, jnp.concatenate(right, 1))
+            if not fresh:
+                total = total + acc[at, :]
             acc[at, :] = total
             return carry
 
         lax.fori_loop(0, count, one_chunk, 0)
+
+    def terms_of(ts, g):
+        return [(t, m, g) for t in ts for m in range(2)]
+
+    crossed = terms_of(crossing, 0) + [(t, 1, 1) for t in crossing]
 
     for copy in loads: copy.wait()
     for g in range(heads): true_keys(g)
@@ -530,6 +550,7 @@
     for j in range(len(chunks)): cross_copy(j).start()
     for g in range(heads): when(b + 2 < n, lambda: key_copy(g).start())
     for g in range(heads): send_near(V, g)
+    for copy in head_loads: copy.start()
     for copy in core_copies + own_copies: copy.start()
     clear()
     for g in range(heads): running_keys(g)
@@ -568,6 +589,7 @@
     send_near_grads(1, 1)
     far_grads(1, 1)
     await_far(V, 0)
+    differentiate_early(0)
     await_near(V, 0)
     join_grads(1, 0)
     differentiate(0)
@@ -575,6 +597,7 @@
     send_near_grads(0, 0)
     hand_on(3)
     await_far(V, 1)
+    differentiate_early(1)
     await_near(V, 1)
     join_grads(1, 1)
     differentiate(1)
@@ -598,19 +621,19 @@
     query_grads(1)
     for copy in own_copies: copy.wait()
     for copy in core_copies: copy.wait_recv()
+    finish(0, 1)
     await_core(0)
-    product((0, 1), 0, True)
-    finish(0, 1)
+    product(terms_of((0, 1), 0), True)
     await_core(1)
-    product((0, 1), 1, False)
-    for m in (1, 0): pass_on(m, 0)
-    await_onward(0)
+    product(terms_of((0, 1), 1), False)
+    for m, g in ((1, 0), (0, 0), (1, 1)): pass_on(m, g)
+    for m, g in ((1, 0), (0, 0), (1, 1)): await_onward(m, g)
     await_thin()
-    product(crossing, 0, False, colour, 1)
-    for m in (1, 0): pass_on(m, 1)
+    product(crossed, False, colour, 1)
+    pass_on(0, 1)
     await_weights()
-    product(crossing, 0, False, 1 - colour, 1)
-    await_onward(1)
+    product(crossed, False, 1 - colour, 1)
+    await_onward(0, 1)
 
     when(b + 1 < n, lambda: near_sum().wait_send())
     for g in range(heads):
@@ -646,11 +669,9 @@
     copies = []
     for c in range(LAST_CHUNKS):
         at = slice(c * chunk, (c + 1) * chunk)
-        total = acc[at, :]
-        for t in range(2, nh):
-            left = jnp.concatenate([weights[t, 0, at, cols], weights[t, 1, at, cols]], 1)
-            right = jnp.concatenate([gathered[t - 1, 0, g], gathered[t - 1, 1, g]], 1)
-            total = total + contract_last(left, right)
+        left = jnp.concatenate([weights[t, 0, at, cols] for t in range(2, nh)], 1)
+        right = jnp.concatenate([gathered[t - 1, 0, g] for t in range(2, nh)], 1)
+        total = acc[at, :] + contract_last(left, right)
         out_ref[at, :] = total.astype(BF16)
         copies.append(pltpu.make_async_copy(out_ref.at[at, :], grad_rows.at[at, :], sem.at[c]))
         copies[-1].start()
@@ -666,6 +687,7 @@
     def local(q, k, v, do, ke, ve, wk, wv):
         tokens, width = k.shape
         heads = width // HEAD_SIZE
+        assert heads == 2
         group = q.shape[1] // width
         tiles = tokens // TILE
         assert ATTEND_WINDOW == 2 * tokens
@@ -703,6 +725,7 @@
                 pltpu.VMEM((heads, 3 * tokens, group * tokens), BF16),
                 pltpu.VMEM((heads, 3, 2, group * tokens), F32),
                 pltpu.VMEM((heads, 3, group * tokens, D), BF16),
+                pltpu.VMEM((heads, 2, tokens, group * tokens), F32),
                 pltpu.VMEM((2, heads, tokens, D), F32),
                 pltpu.VMEM((2, heads, tokens, D), F32),
                 pltpu.VMEM((2, heads, 2, tokens, D), BF16),
@@ -714,7 +737,7 @@
                 dma((n_chunks - 1,)), dma((n_chunks - 1,)), dma((n_chunks - 2, 2)), dma((n_chunks - 2,)), dma((3,)), dma((3,)),
                 dma((2,)), dma((2,)),
                 dma((2,)), dma((2, heads, 2, PIECES)),
-                dma((nh - 1,)), dma((nh - 1, 2, heads)),
+                dma((nh - 1,)), dma((nh - 1, 2, heads)), dma((nh - 1, PIECES)),
             ],
             compiler_params=pltpu.CompilerParams(
                 collective_id=0, has_side_effects=True, vmem_limit_bytes=48 * 2**20

time: 48 us -> 47.8 us (level)
  no operation moved by 1% of the time
where the time goes in v6:
time: 47.8 us; the launch traced here: 47.6 us
  Pallas kernels  46.8 us (98%)
  between operations  0.8 us (2%)
    pallas_call x1, Pallas kernels, local(): pl.pallas_call(functools.partial(kernel, n, nh), out_shape=(pltpu.VMEM(q....  45.4 us
    pallas_call x1, Pallas kernels, local(): pl.pallas_call(functools.partial(last_product, nh, heads), out_shape=(jax...  1.41 us

profile of v6, /device:TPU:0, one launch (start us, length us, event | category | flops | bytes accessed | tf_op | source)
XLA Modules:
  0.0 47.6 jit_solution(17250113853063220506)
XLA Ops:
  0.6 45.4 %shard_map.95 = (bf16[512,512]{1,0:T(8,128)(2,1)S(1)}, bf16[3,2,2,512,128]{4,3,2,1,0:T(8,128)(2,1)S(1)}, bf16[4,2,1344,256]{3,2,1,0:T(8,128)(2,1)S(1)}, f32[1344,512]{1,0:T(8,128)S(1)}) custom-call(bf16[512,512]{1,0:T(8,128)(2,1)} %q_ref.1, bf16[512,256]{1,0:T(8,128)(2,1)} %k_ref.1, bf16[512,256]{1,0:T(8,128)(2,1)} %v_ref.1, bf16[512,512]{1,0:T(8,128)(2,1)} %do_ref.1, ...), custom_call_target="tpu_custom_call" | custom-call | tf_op jit(solution)/shard_map/pallas_call | solution.py:699
  46.0 1.4 %shard_map.96 = (bf16[512,512]{1,0:T(8,128)(2,1)}, bf16[1344,512]{1,0:T(8,128)(2,1)}) custom-call(bf16[512,512]{1,0:T(8,128)(2,1)S(1)} %get-tuple-element.6.dq_ref, bf16[3,2,2,512,128]{4,3,2,1,0:T(8,128)(2,1)S(1)} %get-tuple-element.7.gathered, bf16[4,2,1344,256]{3,2,1,0:T(8,128)(2,1)S(1)} %get-tuple-element.8.weights, f32[1344,512]{1,0:T(8,128)S(1)} %get-tuple-element.9.acc), custom_call_target="tpu_custom_call" | custom-call | tf_op jit(solution)/shard_map/pallas_call | solution.py:746

commit v7 on v6

--- a/solution.py
+++ b/solution.py
@@ -146,7 +146,7 @@
     def cross(t, m, q, j):
         return across(
             w_refs[m].at[pl.ds(partner(h, t) * rows + colour * half + q * part, part), :],
-            held(t, m, q, colour), w_send.at[j], w_recv.at[j], t,
+            held(t, m, q, colour), w_send.at[j // len(chunks)], w_recv.at[j], t,
         )
 
     def cross_copy(j):
@@ -163,28 +163,28 @@
             device_id={"seq": partner(b, 1)}, device_id_type=MESH,
         )
 
-    def chunk_copy(j, step, which):
-        return hand_copy(held(*chunks[j], colour), step, f_send.at[j, which], f_recv.at[j])
+    def chunk_copy(j, step, sent):
+        return hand_copy(held(*chunks[j], colour), step, f_send.at[sent], f_recv.at[j])
 
     def hand(j, action):
         if j < 2:
             when(b >= 2, lambda: action(chunk_copy(j, -2, 0)))
             if j > 0:
-                when(below_top, lambda: action(chunk_copy(j, 2, 1)))
+                when(below_top, lambda: action(chunk_copy(j, 2, 3)))
         else:
             when(b + 2 < n, lambda: action(chunk_copy(j, 2, 1)))
             if j != 3:
-                when(row_0, lambda: action(chunk_copy(j, 0, 0)))
+                when(row_0, lambda: action(chunk_copy(j, 0, 2)))
 
     def hand_on(j):
         cross_copy(j).wait_recv()
         hand(j, lambda copy: copy.start())
 
     def hand_top(action):
-        when(top, lambda: action(chunk_copy(0, 0, 1)))
+        when(top, lambda: action(chunk_copy(0, 0, 4)))
 
     def hand_bottom(action):
-        when(row_1, lambda: action(chunk_copy(3, -2, 0)))
+        when(row_1, lambda: action(chunk_copy(3, -2, 5)))
 
     def thin_copy(which, step, sent, received, side=colour):
         return hand_copy(held(thin_t, thin_m, which, side), step, sent, received)
@@ -212,23 +212,23 @@
 
     def await_weights():
         for j in range(len(chunks)):
-            hand_copy(held(*chunks[j], 1 - colour), 0, f_send.at[j, 0], f_recv.at[j]).wait_recv()
+            hand_copy(held(*chunks[j], 1 - colour), 0, f_send.at[0], f_recv.at[j]).wait_recv()
         thin_side(mine, 1, 1 - colour).wait_recv()
 
     def await_thin():
         thin_side(1 - mine, 2).wait_recv()
 
     core_copies = [
-        across(ref.at[pl.ds(partner(h, 1) * rows, rows), :], weights.at[1, m], c_send.at[m], c_recv.at[m], 1)
+        across(ref.at[pl.ds(partner(h, 1) * rows, rows), :], weights.at[1, m], c_send.at[0], c_recv.at[0], 1)
         for m, ref in enumerate(w_refs)
     ]
     own_copies = [
-        pltpu.make_async_copy(ref.at[pl.ds(h * rows, rows), :], weights.at[0, m], w_own.at[m])
+        pltpu.make_async_copy(ref.at[pl.ds(h * rows, rows), :], weights.at[0, m], w_own.at[0])
         for m, ref in enumerate(w_refs)
     ]
 
     def key_copy(g):
-        return along(key_true.at[g], raw_far.at[g], kf_send.at[g], kf_recv.at[g], 2)
+        return along(key_true.at[g], raw_far.at[g], kf_send.at[0], kf_recv.at[g], 2)
 
     piece = tokens // PIECES
     halo_refs = (value, smooth)
@@ -619,8 +619,8 @@
     query_grads(0)
     finish(0, 0)
     query_grads(1)
-    for copy in own_copies: copy.wait()
-    for copy in core_copies: copy.wait_recv()
+    pltpu.make_async_copy(weights.at[0], weights.at[0], w_own.at[0]).wait()
+    across(weights.at[1], weights.at[1], c_send.at[0], c_recv.at[0], 1).wait_recv()
     finish(0, 1)
     await_core(0)
     product(terms_of((0, 1), 0), True)
@@ -636,8 +636,7 @@
     await_onward(0, 1)
 
     when(b + 1 < n, lambda: near_sum().wait_send())
-    for g in range(heads):
-        when(b + 2 < n, lambda: key_copy(g).wait_send())
+    when(b + 2 < n, lambda: along(key_true, key_true, kf_send.at[0], kf_recv.at[0], 2).wait_send())
     halo = value.at[:, 0:own]
     when(b + 2 < n, lambda: along(halo, halo, h_send.at[FAR], h_recv.at[0, 0, 0, FAR], 2).wait_send())
     when(even | (b >= 2), lambda: along(halo, halo, h_send.at[NEAR], h_recv.at[0, 0, 0, FAR], 2).wait_send())
@@ -650,13 +649,14 @@
     thin_up().wait_send()
     thin_side(mine, 1).wait_send()
     thin_side(1 - mine, 2, 1 - colour).wait_send()
-    for j in range(len(chunks)):
-        cross_copy(j).wait_send()
-        hand(j, lambda copy: copy.wait_send())
+    sent = weights.at[0, :, 0 : len(chunks) * part // 2]
+    across(sent, sent, w_send.at[0], w_recv.at[0], 1).wait_send()
+    for at, condition, count in ((0, b >= 2, 2), (1, b + 2 < n, len(chunks) - 2), (2, row_0, len(chunks) - 3), (3, below_top, 1)):
+        sent = weights.at[0, 0, 0 : count * part]
+        when(condition, lambda: along(sent, sent, f_send.at[at], f_recv.at[0], 2).wait_send())
     hand_top(lambda copy: copy.wait_send())
     hand_bottom(lambda copy: copy.wait_send())
-    for copy in core_copies:
-        copy.wait_send()
+    across(weights.at[1], weights.at[1], c_send.at[0], c_recv.at[0], 1).wait_send()
 
 
 def last_product(nh, heads, dq_ref, gathered, weights, acc, dq_out, grad_rows, out_ref, sem):
@@ -682,7 +682,7 @@
 
 def solution(mesh):
     n, nh = mesh.shape["seq"], mesh.shape["head"]
-    assert n % 8 == 0 and nh >= 4
+    assert n % 8 == 0 and nh == 4
 
     def local(q, k, v, do, ke, ve, wk, wv):
         tokens, width = k.shape
@@ -731,11 +731,11 @@
                 pltpu.VMEM((2, heads, 2, tokens, D), BF16),
                 pltpu.VMEM((2, heads, 2, tokens, D), BF16),
                 pltpu.VMEM((2, heads, tokens, D), BF16),
-                dma((4,)), dma((heads, 2)), dma((2,)),
-                dma((heads,)), dma((heads,)), dma((1,)), dma((1,)),
+                dma((4,)), dma((heads, 2)), dma((1,)),
+                dma((1,)), dma((heads,)), dma((1,)), dma((1,)),
                 dma((2,)), dma((2, heads, PIECES, 2)),
-                dma((n_chunks - 1,)), dma((n_chunks - 1,)), dma((n_chunks - 2, 2)), dma((n_chunks - 2,)), dma((3,)), dma((3,)),
-                dma((2,)), dma((2,)),
+                dma((2,)), dma((n_chunks - 1,)), dma((6,)), dma((n_chunks - 2,)), dma((3,)), dma((3,)),
+                dma((1,)), dma((1,)),
                 dma((2,)), dma((2, heads, 2, PIECES)),
                 dma((nh - 1,)), dma((nh - 1, 2, heads)), dma((nh - 1, PIECES)),
             ],

time: 47.8 us -> 47.7 us (level)
  no operation moved by 1% of the time
where the time goes in v7:
time: 47.7 us; the launch traced here: 47.4 us
  Pallas kernels  46.6 us (98%)
  between operations  0.8 us (2%)
    pallas_call x1, Pallas kernels, local(): pl.pallas_call(functools.partial(kernel, n, nh), out_shape=(pltpu.VMEM(q....  45.2 us
    pallas_call x1, Pallas kernels, local(): pl.pallas_call(functools.partial(last_product, nh, heads), out_shape=(jax...  1.41 us

profile of v7, /device:TPU:0, one launch (start us, length us, event | category | flops | bytes accessed | tf_op | source)
XLA Modules:
  0.0 47.4 jit_solution(5390290212543783881)
XLA Ops:
  0.6 45.2 %shard_map.95 = (bf16[512,512]{1,0:T(8,128)(2,1)S(1)}, bf16[3,2,2,512,128]{4,3,2,1,0:T(8,128)(2,1)S(1)}, bf16[4,2,1344,256]{3,2,1,0:T(8,128)(2,1)S(1)}, f32[1344,512]{1,0:T(8,128)S(1)}) custom-call(bf16[512,512]{1,0:T(8,128)(2,1)} %q_ref.1, bf16[512,256]{1,0:T(8,128)(2,1)} %k_ref.1, bf16[512,256]{1,0:T(8,128)(2,1)} %v_ref.1, bf16[512,512]{1,0:T(8,128)(2,1)} %do_ref.1, ...), custom_call_target="tpu_custom_call" | custom-call | tf_op jit(solution)/shard_map/pallas_call | solution.py:699
  45.8 1.4 %shard_map.96 = (bf16[512,512]{1,0:T(8,128)(2,1)}, bf16[1344,512]{1,0:T(8,128)(2,1)}) custom-call(bf16[512,512]{1,0:T(8,128)(2,1)S(1)} %get-tuple-element.6.dq_ref, bf16[3,2,2,512,128]{4,3,2,1,0:T(8,128)(2,1)S(1)} %get-tuple-element.7.gathered, bf16[4,2,1344,256]{3,2,1,0:T(8,128)(2,1)S(1)} %get-tuple-element.8.weights, f32[1344,512]{1,0:T(8,128)S(1)} %get-tuple-element.9.acc), custom_call_target="tpu_custom_call" | custom-call | tf_op jit(solution)/shard_map/pallas_call | solution.py:746
